TPU v7x, 512 devices: a whole 4x4x16 slice. The times are simulated.
512 devices in a mesh: seq: 64 (over z, x), tp: 8 (over y, core).
Axes of the slice: x: 4, y: 4, z: 16, core: 2. Of those that a mesh axis runs over, the one named last changes fastest.
Arguments:
- queries: bfloat16 [16384, 4096], P(('seq', 'tp')), may hold values from -6 to 6
- key_states: bfloat16 [16384, 2048], P(('seq', 'tp')), may hold values from -6 to 6
- value_state_rows: bfloat16 [16384, 2048], P(('seq', 'tp')), may hold values from -6 to 6
- out_grad: bfloat16 [16384, 4096], P(('seq', 'tp')), may hold values from -6 to 6
- doc_lengths: int32 [16], replicated, may hold values from 1 to 2048, 16384 in all
Outputs:
- query_grad: bfloat16 [16384, 4096], P(('seq', 'tp'))
- key_gradient: bfloat16 [16384, 2048], P(('seq', 'tp'))
- value_gradient: bfloat16 [16384, 2048], P(('seq', 'tp'))
Inputs may be any that keep to these rules, and one draw needn't show every extreme that they name: `doc_lengths`: the documents lie one after another from position 0 and fill all 16384 positions; the longest has exactly 2048 tokens.
All inputs are finite; a program needn't handle non-finite values.
Results may differ from a plain program's by a relative error of at most 0.013.
Values may be sent and summed in bfloat16 or wider, within the bound.
A program may use at most 64 MiB of HBM per device.

v0:
```python
import jax
import jax.numpy as jnp
from jax import lax
from jax.sharding import PartitionSpec as P

QUERY_HEADS = 32
KEY_HEADS = 16
HEAD_SIZE = 128
WINDOW = 1024


attn_scale = 168.0 ** (-0.5)
masked_floor = -1e30


def passed_along(value, axis, steps):
    count = lax.axis_size(axis)
    initial, last = (max(0, -steps), min(count, count - steps))
    return lax.ppermute(value, axis, [(source, source + steps) for source in range(initial, last)])


def run_stretch(stretch_index, work):
    if stretch_index == 0:
        return work()
    return work()


def per_device(queries, key_states, value_state_rows, out_grad, doc_lengths):
    query_matrix, key_matrix, value_matrix, grad_all = (
        lax.all_to_all(queries, "tp", split_axis=1, concat_axis=0, tiled=True),
        lax.all_to_all(key_states, "tp", split_axis=1, concat_axis=0, tiled=True),
        lax.all_to_all(value_state_rows, "tp", split_axis=1, concat_axis=0, tiled=True),
        lax.all_to_all(out_grad, "tp", split_axis=1, concat_axis=0, tiled=True),
    )
    stretch_rows = query_matrix.shape[0]
    kv_local = key_matrix.shape[1] // HEAD_SIZE
    group_width = QUERY_HEADS // KEY_HEADS
    halo_count = WINDOW // stretch_rows
    stretch_first = lax.axis_index("seq") * stretch_rows
    starts_arr = jnp.cumsum(doc_lengths) - doc_lengths

    def doc_of(positions):
        counted = jnp.sum((starts_arr[None, :] <= positions[:, None]).astype(jnp.int32), axis=1)
        return counted - 1

    offsets = jnp.arange(stretch_rows, dtype=jnp.int32)
    query_pos = stretch_first + offsets
    query_doc = doc_of(query_pos)
    query_four = query_matrix.reshape(stretch_rows, kv_local, group_width, HEAD_SIZE)
    grad_four = grad_all.reshape(stretch_rows, kv_local, group_width, HEAD_SIZE)
    kv_pair = jnp.stack([key_matrix, value_matrix])
    stretches = [kv_pair]
    for distance in range(1, halo_count + 1):
        stretches.append(passed_along(kv_pair, "seq", distance))

    def visible(stretch_index):
        key_pos = stretch_first - stretch_index * stretch_rows + offsets
        allowed = (key_pos[None, :] <= query_pos[:, None]) & (
            query_pos[:, None] - key_pos[None, :] < WINDOW
        )
        allowed = allowed & (key_pos[None, :] >= 0)
        allowed = allowed & (doc_of(key_pos)[None, :] == query_doc[:, None])
        return allowed[None, None, :, :]

    def split_pair(pair):
        return (
            pair[0].reshape(stretch_rows, kv_local, HEAD_SIZE),
            pair[1].reshape(stretch_rows, kv_local, HEAD_SIZE),
        )

    def scores_of(key_tile):
        return (
            jnp.einsum("qgrd,kgd->grqk", query_four, key_tile, preferred_element_type=jnp.float32)
            * attn_scale
        )

    stat_shape = (kv_local, group_width, stretch_rows)
    maxima = []
    totals = []
    for stretch_index in range(halo_count + 1):

        def stats_work(pair=stretches[stretch_index], stretch_index=stretch_index):
            key_tile, value_tile = split_pair(pair)
            allowed = visible(stretch_index)
            raw_scores = scores_of(key_tile)
            row_max = jnp.max(jnp.where(allowed, raw_scores, masked_floor), axis=-1)
            row_sum = jnp.sum(
                jnp.where(allowed, jnp.exp(raw_scores - row_max[..., None]), 0.0), axis=-1
            )
            return (row_max, row_sum)

        row_max, row_sum = run_stretch(stretch_index, stats_work)
        maxima.append(row_max)
        totals.append(row_sum)
    peak_max = maxima[0]
    for row_max in maxima[1:]:
        peak_max = jnp.maximum(peak_max, row_max)
    norm_sum = jnp.zeros(stat_shape, jnp.float32)
    for row_max, row_sum in zip(maxima, totals):
        norm_sum = norm_sum + row_sum * jnp.exp(row_max - peak_max)
    log_total = peak_max + jnp.log(norm_sum)

    def probs_of(raw_scores, allowed):
        return jnp.where(allowed, jnp.exp(raw_scores - log_total[..., None]), 0.0)

    out_shape = (stretch_rows, kv_local, group_width, HEAD_SIZE)
    attn_out = jnp.zeros(out_shape, jnp.float32)
    for stretch_index in range(halo_count + 1):

        def output_work(pair=stretches[stretch_index], stretch_index=stretch_index):
            key_tile, value_tile = split_pair(pair)
            probs_bf = probs_of(scores_of(key_tile), visible(stretch_index)).astype(jnp.bfloat16)
            return jnp.einsum(
                "grqk,kgd->qgrd", probs_bf, value_tile, preferred_element_type=jnp.float32
            )

        attn_out = attn_out + run_stretch(stretch_index, output_work)
    delta_rows = jnp.transpose(
        jnp.sum(grad_four.astype(jnp.float32) * attn_out, axis=-1), (1, 2, 0)
    )
    query_sum = jnp.zeros(out_shape, jnp.float32)
    terms = []
    for stretch_index in range(halo_count + 1):

        def grad_work(pair=stretches[stretch_index], stretch_index=stretch_index):
            key_tile, value_tile = split_pair(pair)
            probs = probs_of(scores_of(key_tile), visible(stretch_index))
            probs_bf = probs.astype(jnp.bfloat16)
            prob_grad = jnp.einsum(
                "qgrd,kgd->grqk", grad_four, value_tile, preferred_element_type=jnp.float32
            )
            grad_scores = (probs * (prob_grad - delta_rows[..., None]) * attn_scale).astype(
                jnp.bfloat16
            )
            query_part = jnp.einsum(
                "grqk,kgd->qgrd", grad_scores, key_tile, preferred_element_type=jnp.float32
            )
            key_part = jnp.einsum(
                "grqk,qgrd->kgd", grad_scores, query_four, preferred_element_type=jnp.float32
            )
            value_part = jnp.einsum(
                "grqk,qgrd->kgd", probs_bf, grad_four, preferred_element_type=jnp.float32
            )
            stacked = jnp.stack(
                [
                    key_part.reshape(stretch_rows, kv_local * HEAD_SIZE),
                    value_part.reshape(stretch_rows, kv_local * HEAD_SIZE),
                ]
            )
            return (query_part, stacked)

        query_part, stacked = run_stretch(stretch_index, grad_work)
        query_sum = query_sum + query_part
        terms.append(stacked)
    summed = terms[0]
    for distance in range(1, halo_count + 1):
        summed = summed + passed_along(terms[distance], "seq", -distance)
    query_grad = query_sum.reshape(stretch_rows, kv_local * group_width * HEAD_SIZE).astype(
        jnp.bfloat16
    )
    key_gradient = summed[0].astype(jnp.bfloat16)
    value_gradient = summed[1].astype(jnp.bfloat16)
    return (
        lax.all_to_all(query_grad, "tp", split_axis=0, concat_axis=1, tiled=True),
        lax.all_to_all(key_gradient, "tp", split_axis=0, concat_axis=1, tiled=True),
        lax.all_to_all(value_gradient, "tp", split_axis=0, concat_axis=1, tiled=True),
    )


def solution(mesh):
    return jax.shard_map(
        per_device,
        mesh=mesh,
        in_specs=(
            P(("seq", "tp"), None),
            P(("seq", "tp"), None),
            P(("seq", "tp"), None),
            P(("seq", "tp"), None),
            P(),
        ),
        out_specs=(P(("seq", "tp"), None), P(("seq", "tp"), None), P(("seq", "tp"), None)),
        check_vma=False,
    )
```

profile of v0, /device:TPU:1, one launch (start us, length us, event | category | flops | bytes accessed | tf_op | source)
XLA Modules:
  0.0 177.2 jit_solution(2559601820198829223)
XLA Ops:
  0.6 1.6 copy.492
  2.2 10.2 %all-to-all-start = ((bf16[32,8,256]{2,0,1:T(8,128)(2,1)}), bf16[32,8,256]{2,0,1:T(8,128)(2,1)S(1)}, u32[]{:S(2)}, u32[]{:S(2)}) async-start(bf16[32,8,256]{2,0,1:T(8,128)(2,1)} %bitcast.314), calls=%async_computation | async-start | bytes 262144 | tf_op jit(solution)/shard_map/all_to_all | solution.py:31
  14.2 3.5 %all-to-all-done = bf16[32,8,256]{2,0,1:T(8,128)(2,1)S(1)} async-done(((bf16[32,8,256]{2,0,1:T(8,128)(2,1)}), bf16[32,8,256]{2,0,1:T(8,128)(2,1)S(1)}, u32[]{:S(2)}, u32[]{:S(2)}) %all-to-all-start) | async-done | bytes 131104 | tf_op jit(solution)/shard_map/all_to_all | solution.py:31
  17.7 4.1 %all-to-all-start.2 = ((bf16[32,8,256]{2,0,1:T(8,128)(2,1)}), bf16[32,8,256]{2,0,1:T(8,128)(2,1)S(1)}, u32[]{:S(2)}, u32[]{:S(2)}) async-start(bf16[32,8,256]{2,0,1:T(8,128)(2,1)} %bitcast.313), calls=%async_computation.2 | async-start | bytes 262144 | tf_op jit(solution)/shard_map/all_to_all | solution.py:32
  22.6 4.5 %all-to-all-done.2 = bf16[32,8,256]{2,0,1:T(8,128)(2,1)S(1)} async-done(((bf16[32,8,256]{2,0,1:T(8,128)(2,1)}), bf16[32,8,256]{2,0,1:T(8,128)(2,1)S(1)}, u32[]{:S(2)}, u32[]{:S(2)}) %all-to-all-start.2) | async-done | bytes 131104 | tf_op jit(solution)/shard_map/all_to_all | solution.py:32
  27.1 4.2 %all-to-all-start.1 = ((bf16[32,8,512]{2,0,1:T(8,128)(2,1)}), bf16[32,8,512]{2,0,1:T(8,128)(2,1)S(1)}, u32[]{:S(2)}, u32[]{:S(2)}) async-start(bf16[32,8,512]{2,0,1:T(8,128)(2,1)} %bitcast.312), calls=%async_computation.1 | async-start | bytes 524288 | tf_op jit(solution)/shard_map/all_to_all | solution.py:30
  33.4 2.0 %collective-permute-start = (bf16[2,256,256]{2,1,0:T(8,128)(2,1)S(1)}, bf16[2,256,256]{2,1,0:T(8,128)(2,1)}, u32[]{:S(2)}, u32[]{:S(2)}) collective-permute-start(bf16[2,256,256]{2,1,0:T(8,128)(2,1)S(1)} %pad_maximum_fusion.4), channel_id=1, source_target_pairs={{0,8},{8,16},{16,24},{24,32},{32,40},{40,48},{48,56},{56,64},{64,7... | collective-permute-start | bytes 786440 | tf_op jit(solution)/shard_map/ppermute | solution.py:19
  36.7 4.4 %collective-permute-start.2 = (bf16[2,256,256]{2,1,0:T(8,128)(2,1)S(1)}, bf16[2,256,256]{2,1,0:T(8,128)(2,1)S(1)}, u32[]{:S(2)}, u32[]{:S(2)}) collective-permute-start(bf16[2,256,256]{2,1,0:T(8,128)(2,1)S(1)} %pad_maximum_fusion.4), channel_id=1, source_target_pairs={{0,24},{8,32},{16,40},{24,48},{32,56},{40,64},{48,72},{56,80},{64,... | collective-permute-start | bytes 786440 | tf_op jit(solution)/shard_map/ppermute | solution.py:19
  41.1 3.5 %collective-permute-start.3 = (bf16[2,256,256]{2,1,0:T(8,128)(2,1)S(1)}, bf16[2,256,256]{2,1,0:T(8,128)(2,1)S(1)}, u32[]{:S(2)}, u32[]{:S(2)}) collective-permute-start(bf16[2,256,256]{2,1,0:T(8,128)(2,1)S(1)} %pad_maximum_fusion.4), channel_id=1, source_target_pairs={{0,32},{8,40},{16,48},{24,56},{32,64},{40,72},{48,80},{56,88},{64,... | collective-permute-start | bytes 786440 | tf_op jit(solution)/shard_map/ppermute | solution.py:19
  45.6 5.9 %all-to-all-start.3 = ((bf16[32,8,512]{2,0,1:T(8,128)(2,1)}), bf16[32,8,512]{2,0,1:T(8,128)(2,1)S(1)}, u32[]{:S(2)}, u32[]{:S(2)}) async-start(bf16[32,8,512]{2,0,1:T(8,128)(2,1)} %bitcast.311), calls=%async_computation.3 | async-start | bytes 524288 | tf_op jit(solution)/shard_map/all_to_all | solution.py:33
  52.3 5.7 %all-to-all-done.3 = bf16[32,8,512]{2,0,1:T(8,128)(2,1)S(1)} async-done(((bf16[32,8,512]{2,0,1:T(8,128)(2,1)}), bf16[32,8,512]{2,0,1:T(8,128)(2,1)S(1)}, u32[]{:S(2)}, u32[]{:S(2)}) %all-to-all-start.3) | async-done | bytes 262176 | tf_op jit(solution)/shard_map/all_to_all | solution.py:33
  58.9 1.6 fusion.88
  73.0 1.7 copy.338
  74.6 2.3 %convolution_bitcast_fusion.12 = f32[256,2,2,128]{0,3,2,1:T(8,128)} fusion(bf16[256,2,128,1]{0,2,3,1:T(8,128)(2,1)} %bitcast.348, f32[2,2,256,256]{2,3,1,0:T(8,128)} %copy-done, f32[2,2,256]{2,1,0:T(2,128)S(1)} %log_add_fusion, pred[256,256]{0,1:T(8,128)(4,1)} %get-tuple-element.20), kind=kOutput, calls=%fused_computation.42 | convolution fusion | flops 67895296 | bytes 1773568 | tf_op jit(solution)/shard_map/grqk,kgd->qgrd/dot_general | solution.py:113
  77.0 1.6 copy.340
  78.6 2.4 %convolution_bitcast_fusion.11 = f32[256,2,2,128]{0,3,2,1:T(8,128)} fusion(bf16[256,2,128,1]{0,2,3,1:T(8,128)(2,1)} %bitcast.346, f32[2,2,256,256]{2,3,1,0:T(8,128)} %copy-done.2, f32[2,2,256]{2,1,0:T(2,128)S(1)} %log_add_fusion, pred[256,256]{0,1:T(8,128)(4,1)} %get-tuple-element.21), kind=kOutput, calls=%fused_computation.41 | convolution fusion | flops 67895296 | bytes 1773568 | tf_op jit(solution)/shard_map/grqk,kgd->qgrd/dot_general | solution.py:113
  81.0 1.7 copy.334
  82.6 2.1 %fusion.71 = f32[2,256,128,1]{1,2,3,0:T(8,128)} fusion(bf16[256,2,2,128]{0,3,2,1:T(8,128)(2,1)} %copy.331, f32[2,2,256,256]{2,3,1,0:T(8,128)S(1)} %get-tuple-element.30, f32[2,2,256]{2,1,0:T(2,128)S(1)} %log_add_fusion, pred[256,256]{0,1:T(8,128)(4,1)S(1)} %get-tuple-element.22), kind=kOutput, calls=%fused_computation.115 | convolution fusion | flops 67895296 | bytes 1642496 | tf_op jit(solution)/shard_map/grqk,qgrd->kgd/dot_general | solution.py:141
  84.8 1.6 fusion.35
  98.9 1.8 %copy.372 = f32[1,256,256]{2,1,0:T(8,128)} copy(f32[1,256,256]{1,2,0:T(8,128)} %bitcast.341) | data formatting | bytes 524288 | tf_op jit(solution)/shard_map/stack;reshape | solution.py:144
  101.5 1.9 %pad_maximum_fusion = f32[2,256,256]{2,1,0:T(8,128)} fusion(f32[1,256,256]{2,1,0:T(8,128)} %copy.373, f32[1,256,256]{2,1,0:T(8,128)} %copy.372), kind=kLoop, calls=%fused_computation.81 | loop fusion | flops 131072 | bytes 1048576 | tf_op jit(solution)/shard_map/stack | solution.py:144
  104.7 1.8 %copy.378 = f32[1,256,256]{2,1,0:T(8,128)} copy(f32[1,256,256]{1,2,0:T(8,128)} %bitcast.339) | data formatting | bytes 524288 | tf_op jit(solution)/shard_map/stack;reshape | solution.py:144
  107.3 1.9 %pad_maximum_fusion.1 = f32[2,256,256]{2,1,0:T(8,128)} fusion(f32[1,256,256]{2,1,0:T(8,128)} %copy.379, f32[1,256,256]{2,1,0:T(8,128)} %copy.378), kind=kLoop, calls=%fused_computation.82 | loop fusion | flops 131072 | bytes 1048576 | tf_op jit(solution)/shard_map/stack | solution.py:144
  112.4 1.8 %pad_maximum_fusion.2 = f32[2,256,256]{2,1,0:T(8,128)} fusion(f32[1,256,256]{2,1,0:T(8,128)S(1)} %copy-done.29, f32[1,256,256]{2,1,0:T(8,128)} %copy.384), kind=kLoop, calls=%fused_computation.83 | loop fusion | flops 131072 | bytes 1048576 | tf_op jit(solution)/shard_map/stack | solution.py:144
  121.7 4.4 %all-to-all-start.4 = ((bf16[8,32,512]{2,1,0:T(8,128)(2,1)}), bf16[8,32,512]{2,1,0:T(8,128)(2,1)S(1)}, u32[]{:S(2)}, u32[]{:S(2)}) async-start(bf16[8,32,512]{2,1,0:T(8,128)(2,1)} %convert_element_type.98), calls=%async_computation.4 | async-start | bytes 524288 | tf_op jit(solution)/shard_map/all_to_all | solution.py:164
  126.1 9.0 %collective-permute-done.5 = f32[2,256,256]{2,1,0:T(8,128)} collective-permute-done((f32[2,256,256]{2,1,0:T(8,128)}, f32[2,256,256]{2,1,0:T(8,128)}, u32[]{:S(2)}, u32[]{:S(2)}) %collective-permute-start.5) | collective-permute-done | bytes 524320 | tf_op jit(solution)/shard_map/ppermute | solution.py:19
  135.1 2.6 %collective-permute-done.6 = f32[2,256,256]{2,1,0:T(8,128)} collective-permute-done((f32[2,256,256]{2,1,0:T(8,128)}, f32[2,256,256]{2,1,0:T(8,128)}, u32[]{:S(2)}, u32[]{:S(2)}) %collective-permute-start.6) | collective-permute-done | bytes 524320 | tf_op jit(solution)/shard_map/ppermute | solution.py:19
  137.8 17.0 %collective-permute-done.7 = f32[2,256,256]{2,1,0:T(8,128)} collective-permute-done((f32[2,256,256]{2,1,0:T(8,128)}, f32[2,256,256]{2,1,0:T(8,128)}, u32[]{:S(2)}, u32[]{:S(2)}) %collective-permute-start.7) | collective-permute-done | bytes 524320 | tf_op jit(solution)/shard_map/ppermute | solution.py:19
  154.8 1.7 fusion.44
  157.1 10.0 %all_to_all.112 = bf16[8,32,256]{2,1,0:T(8,128)(2,1)S(1)} all-to-all(bf16[8,32,256]{2,1,0:T(8,128)(2,1)S(1)} %bitcast.353), channel_id=1, replica_groups=mesh['seq'=64,'tp'=8] {'tp'}, dimensions={0} | all-to-all | bytes 262144 | tf_op jit(solution)/shard_map/all_to_all | solution.py:165
  167.2 4.1 %all-to-all-start.6 = ((bf16[8,32,256]{2,1,0:T(8,128)(2,1)}), bf16[8,32,256]{2,1,0:T(8,128)(2,1)S(1)}, u32[]{:S(2)}, u32[]{:S(2)}) async-start(bf16[8,32,256]{2,1,0:T(8,128)(2,1)} %bitcast.107), calls=%async_computation.6 | async-start | bytes 262144 | tf_op jit(solution)/shard_map/all_to_all | solution.py:166
  172.7 3.9 %all-to-all-done.6 = bf16[8,32,256]{2,1,0:T(8,128)(2,1)S(1)} async-done(((bf16[8,32,256]{2,1,0:T(8,128)(2,1)}), bf16[8,32,256]{2,1,0:T(8,128)(2,1)S(1)}, u32[]{:S(2)}, u32[]{:S(2)}) %all-to-all-start.6) | async-done | bytes 131104 | tf_op jit(solution)/shard_map/all_to_all | solution.py:166
  (177 shorter events, 49.4 us)
Async XLA Ops:
  2.2 11.3 %copy-start.39 = (bf16[32,2048]{1,0:T(8,128)(2,1)S(1)}, bf16[32,2048]{1,0:T(8,128)(2,1)}, u32[]{:S(2)}) copy-start(bf16[32,2048]{1,0:T(8,128)(2,1)} %param.7) | copy-start | bytes 393220
  2.2 15.5 %all-to-all-start = ((bf16[32,8,256]{2,0,1:T(8,128)(2,1)}), bf16[32,8,256]{2,0,1:T(8,128)(2,1)S(1)}, u32[]{:S(2)}, u32[]{:S(2)}) async-start(bf16[32,8,256]{2,0,1:T(8,128)(2,1)} %bitcast.314), calls=%async_computation | async-start | bytes 262144 | tf_op jit(solution)/shard_map/all_to_all | solution.py:31
  13.5 8.3 %copy-start.37 = (bf16[32,4096]{1,0:T(8,128)(2,1)S(1)}, bf16[32,4096]{1,0:T(8,128)(2,1)}, u32[]{:S(2)}) copy-start(bf16[32,4096]{1,0:T(8,128)(2,1)} %param.5) | copy-start | bytes 786436
  17.7 9.4 %all-to-all-start.2 = ((bf16[32,8,256]{2,0,1:T(8,128)(2,1)}), bf16[32,8,256]{2,0,1:T(8,128)(2,1)S(1)}, u32[]{:S(2)}, u32[]{:S(2)}) async-start(bf16[32,8,256]{2,0,1:T(8,128)(2,1)} %bitcast.313), calls=%async_computation.2 | async-start | bytes 262144 | tf_op jit(solution)/shard_map/all_to_all | solution.py:32
  27.1 18.4 %all-to-all-start.1 = ((bf16[32,8,512]{2,0,1:T(8,128)(2,1)}), bf16[32,8,512]{2,0,1:T(8,128)(2,1)S(1)}, u32[]{:S(2)}, u32[]{:S(2)}) async-start(bf16[32,8,512]{2,0,1:T(8,128)(2,1)} %bitcast.312), calls=%async_computation.1 | async-start | bytes 524288 | tf_op jit(solution)/shard_map/all_to_all | solution.py:30
  31.3 1.3 copy-start.38
  33.4 25.5 %collective-permute-start = (bf16[2,256,256]{2,1,0:T(8,128)(2,1)S(1)}, bf16[2,256,256]{2,1,0:T(8,128)(2,1)}, u32[]{:S(2)}, u32[]{:S(2)}) collective-permute-start(bf16[2,256,256]{2,1,0:T(8,128)(2,1)S(1)} %pad_maximum_fusion.4), channel_id=1, source_target_pairs={{0,8},{8,16},{16,24},{24,32},{32,40},{40,48},{48,56},{56,64},{64,7... | collective-permute-start | bytes 786440 | tf_op jit(solution)/shard_map/ppermute | solution.py:19
  35.4 25.2 %collective-permute-start.1 = (bf16[2,256,256]{2,1,0:T(8,128)(2,1)S(1)}, bf16[2,256,256]{2,1,0:T(8,128)(2,1)S(1)}, u32[]{:S(2)}, u32[]{:S(2)}) collective-permute-start(bf16[2,256,256]{2,1,0:T(8,128)(2,1)S(1)} %pad_maximum_fusion.4), channel_id=1, source_target_pairs={{0,16},{8,24},{16,32},{24,40},{32,48},{40,56},{48,64},{56,72},{64,... | collective-permute-start | bytes 786440 | tf_op jit(solution)/shard_map/ppermute | solution.py:19
  36.7 24.7 %collective-permute-start.2 = (bf16[2,256,256]{2,1,0:T(8,128)(2,1)S(1)}, bf16[2,256,256]{2,1,0:T(8,128)(2,1)S(1)}, u32[]{:S(2)}, u32[]{:S(2)}) collective-permute-start(bf16[2,256,256]{2,1,0:T(8,128)(2,1)S(1)} %pad_maximum_fusion.4), channel_id=1, source_target_pairs={{0,24},{8,32},{16,40},{24,48},{32,56},{40,64},{48,72},{56,80},{64,... | collective-permute-start | bytes 786440 | tf_op jit(solution)/shard_map/ppermute | solution.py:19
  41.1 21.7 %collective-permute-start.3 = (bf16[2,256,256]{2,1,0:T(8,128)(2,1)S(1)}, bf16[2,256,256]{2,1,0:T(8,128)(2,1)S(1)}, u32[]{:S(2)}, u32[]{:S(2)}) collective-permute-start(bf16[2,256,256]{2,1,0:T(8,128)(2,1)S(1)} %pad_maximum_fusion.4), channel_id=1, source_target_pairs={{0,32},{8,40},{16,48},{24,56},{32,64},{40,72},{48,80},{56,88},{64,... | collective-permute-start | bytes 786440 | tf_op jit(solution)/shard_map/ppermute | solution.py:19
  44.7 7.0 %copy-start.17 = (bf16[256,2,128]{2,1,0:T(2,128)(2,1)}, bf16[256,2,128]{2,1,0:T(2,128)(2,1)S(1)}, u32[]{:S(2)}) copy-start(bf16[256,2,128]{2,1,0:T(2,128)(2,1)S(1)} %reshape_squeeze_stack.4) | copy-start | bytes 393220
  45.6 12.4 %all-to-all-start.3 = ((bf16[32,8,512]{2,0,1:T(8,128)(2,1)}), bf16[32,8,512]{2,0,1:T(8,128)(2,1)S(1)}, u32[]{:S(2)}, u32[]{:S(2)}) async-start(bf16[32,8,512]{2,0,1:T(8,128)(2,1)} %bitcast.311), calls=%async_computation.3 | async-start | bytes 524288 | tf_op jit(solution)/shard_map/all_to_all | solution.py:33
  60.7 4.4 %copy-start.15 = (bf16[1,256,256]{1,2,0:T(8,128)(2,1)}, bf16[1,256,256]{1,2,0:T(8,128)(2,1)S(1)}, u32[]{:S(2)}) copy-start(bf16[1,256,256]{1,2,0:T(8,128)(2,1)S(1)} %copy.316) | copy-start | bytes 393220
  68.1 1.5 copy-start
  69.7 2.2 %copy-start.2 = (f32[2,2,256,256]{2,3,1,0:T(8,128)}, f32[2,2,256,256]{2,3,1,0:T(8,128)S(1)}, u32[]{:S(2)}) copy-start(f32[2,2,256,256]{2,3,1,0:T(8,128)S(1)} %get-tuple-element.24) | copy-start | bytes 3145732
  82.6 2.1 %copy-start.4 = (bf16[256,2,2,128]{0,3,2,1:T(8,128)(2,1)S(1)}, bf16[256,2,2,128]{0,3,2,1:T(8,128)(2,1)}, u32[]{:S(2)}) copy-start(bf16[256,2,2,128]{0,3,2,1:T(8,128)(2,1)} %copy.331) | copy-start | bytes 786436
  82.6 2.1 %copy-start.5 = (f32[256,2,2,128]{0,3,2,1:T(8,128)S(1)}, f32[256,2,2,128]{0,3,2,1:T(8,128)}, u32[]{:S(2)}) copy-start(f32[256,2,2,128]{0,3,2,1:T(8,128)} %convolution_bitcast_fusion.5) | copy-start | bytes 1572868
  82.6 2.1 %copy-start.6 = (f32[256,2,2,128]{0,3,2,1:T(8,128)S(1)}, f32[256,2,2,128]{0,3,2,1:T(8,128)}, u32[]{:S(2)}) copy-start(f32[256,2,2,128]{0,3,2,1:T(8,128)} %convolution_bitcast_fusion.13) | copy-start | bytes 1572868
  82.6 2.1 %copy-start.30 = (bf16[1,256,256]{1,2,0:T(8,128)(2,1)S(1)}, bf16[1,256,256]{1,2,0:T(8,128)(2,1)}, u32[]{:S(2)}) copy-start(bf16[1,256,256]{1,2,0:T(8,128)(2,1)} %copy.334) | copy-start | bytes 393220
  87.3 10.6 %copy-start.7 = (bf16[2,2,256,256]{2,3,1,0:T(8,128)(2,1)}, bf16[2,2,256,256]{2,3,1,0:T(8,128)(2,1)S(1)}, u32[]{:S(2)}) copy-start(bf16[2,2,256,256]{2,3,1,0:T(8,128)(2,1)S(1)} %fusion.23) | copy-start | bytes 1572868
  87.7 1.2 copy-start.1
  89.9 1.2 copy-start.3
  89.9 1.2 copy-start.10
  98.9 1.8 %copy-start.25 = (f32[2,256,128,1]{1,2,3,0:T(8,128)S(1)}, f32[2,256,128,1]{1,2,3,0:T(8,128)}, u32[]{:S(2)}) copy-start(f32[2,256,128,1]{1,2,3,0:T(8,128)} %fusion.71) | copy-start | bytes 786436
  103.4 22.7 %collective-permute-start.4 = (f32[2,256,256]{2,1,0:T(8,128)}, f32[2,256,256]{2,1,0:T(8,128)}, u32[]{:S(2)}, u32[]{:S(2)}) collective-permute-start(f32[2,256,256]{2,1,0:T(8,128)} %pad_maximum_fusion), channel_id=1, source_target_pairs={{8,0},{16,8},{24,16},{32,24},{40,32},{48,40},{56,48},{64,56},{72,6... | collective-permute-start | bytes 1572872 | tf_op jit(solution)/shard_map/ppermute | solution.py:19
  104.7 1.8 %copy-start.26 = (f32[2,256,128,1]{1,2,3,0:T(8,128)S(1)}, f32[2,256,128,1]{1,2,3,0:T(8,128)}, u32[]{:S(2)}) copy-start(f32[2,256,128,1]{1,2,3,0:T(8,128)} %fusion.68) | copy-start | bytes 786436
  109.2 25.9 %collective-permute-start.5 = (f32[2,256,256]{2,1,0:T(8,128)}, f32[2,256,256]{2,1,0:T(8,128)}, u32[]{:S(2)}, u32[]{:S(2)}) collective-permute-start(f32[2,256,256]{2,1,0:T(8,128)} %pad_maximum_fusion.1), channel_id=1, source_target_pairs={{16,0},{24,8},{32,16},{40,24},{48,32},{56,40},{64,48},{72,56},{80,... | collective-permute-start | bytes 1572872 | tf_op jit(solution)/shard_map/ppermute | solution.py:19
  114.2 23.6 %collective-permute-start.6 = (f32[2,256,256]{2,1,0:T(8,128)}, f32[2,256,256]{2,1,0:T(8,128)}, u32[]{:S(2)}, u32[]{:S(2)}) collective-permute-start(f32[2,256,256]{2,1,0:T(8,128)} %pad_maximum_fusion.2), channel_id=1, source_target_pairs={{24,0},{32,8},{40,16},{48,24},{56,32},{64,40},{72,48},{80,56},{88,... | collective-permute-start | bytes 1572872 | tf_op jit(solution)/shard_map/ppermute | solution.py:19
  116.0 2.1 %copy-start.27 = (f32[2,256,128,1]{1,2,3,0:T(8,128)S(1)}, f32[2,256,128,1]{1,2,3,0:T(8,128)}, u32[]{:S(2)}) copy-start(f32[2,256,128,1]{1,2,3,0:T(8,128)} %fusion.92) | copy-start | bytes 786436
  116.9 37.9 %collective-permute-start.7 = (f32[2,256,256]{2,1,0:T(8,128)}, f32[2,256,256]{2,1,0:T(8,128)}, u32[]{:S(2)}, u32[]{:S(2)}) collective-permute-start(f32[2,256,256]{2,1,0:T(8,128)} %pad_maximum_fusion.3), channel_id=1, source_target_pairs={{32,0},{40,8},{48,16},{56,24},{64,32},{72,40},{80,48},{88,56},{96,... | collective-permute-start | bytes 1572872 | tf_op jit(solution)/shard_map/ppermute | solution.py:19
  121.7 35.4 %all-to-all-start.4 = ((bf16[8,32,512]{2,1,0:T(8,128)(2,1)}), bf16[8,32,512]{2,1,0:T(8,128)(2,1)S(1)}, u32[]{:S(2)}, u32[]{:S(2)}) async-start(bf16[8,32,512]{2,1,0:T(8,128)(2,1)} %convert_element_type.98), calls=%async_computation.4 | async-start | bytes 524288 | tf_op jit(solution)/shard_map/all_to_all | solution.py:164
  167.2 9.4 %all-to-all-start.6 = ((bf16[8,32,256]{2,1,0:T(8,128)(2,1)}), bf16[8,32,256]{2,1,0:T(8,128)(2,1)S(1)}, u32[]{:S(2)}, u32[]{:S(2)}) async-start(bf16[8,32,256]{2,1,0:T(8,128)(2,1)} %bitcast.107), calls=%async_computation.6 | async-start | bytes 262144 | tf_op jit(solution)/shard_map/all_to_all | solution.py:166
  (23 other events, 22.1 us)
where the time goes:
time: 179 us; the launch traced here: 177 us
  starting transfers between devices  49.4 us (28%)
  waiting for transfers between devices  46.3 us (26%)
  local copies, waits for them, and re-layouts  36.7 us (21%)
  matrix products  22.8 us (13%)
  other arithmetic  10.7 us (6%)
  blocking collectives  10 us (6%)
    ppermute x8, waiting for transfers between devices, passed_along(): lax.ppermute(value, axis, [(source, source + steps) for source in range(i...  28.7 us
    ppermute x8, starting transfers between devices, passed_along(): lax.ppermute(value, axis, [(source, source + steps) for source in range(i...  16.4 us
    all_to_all x1, starting transfers between devices, per_device(): lax.all_to_all(key_states, 'tp', split_axis=1, concat_axis=0, tiled=True)  10.2 us
    all_to_all x1, blocking collectives, per_device(): lax.all_to_all(key_gradient, 'tp', split_axis=0, concat_axis=1, tiled=True)  10 us
    slice x8, local copies, waits for them, and re-layouts, split_pair(): pair[1].reshape(stretch_rows, kv_local, HEAD_SIZE)  8.73 us
    unnamed x82, local copies, waits for them, and re-layouts  8.57 us
    dot_general x5, matrix products, output_work(): jnp.einsum('grqk,kgd->qgrd', probs_bf, value_tile, preferred_element_type...  8.5 us
    another operation x10, local copies, waits for them, and re-layouts, grad_work(): jnp.stack([key_part.reshape(stretch_rows, kv_local * HEAD_SIZE), value_pa...  7.5 us
  transfers between devices with their start and end apart: 14, of which 7 were waited for; matrix products, arithmetic and copies ran while one was open for 14% of the time, Pallas kernels for 0%

commit v1 on v0

v1 whole, which is shorter than its diff:
```python
import functools
import math

import jax
import jax.numpy as jnp
from jax import lax
from jax.experimental import pallas as pl
from jax.experimental.pallas import tpu as pltpu
from jax.sharding import PartitionSpec as P

MESH = pl.DeviceIdType.MESH
HEAD = 128
ROWS = 32
HALF = 512
BLOCK = 256
SPAN = 3 * HALF
WINDOW = 1024
DOCS = 16
SCALE = 168.0 ** (-0.5)
EXP_SCALE = SCALE / math.log(2.0)
FLOOR = -1e30
BF = jnp.bfloat16
F32 = jnp.float32


def dot_nt(a, b):
    return lax.dot_general(a, b, (((1,), (1,)), ((), ())), preferred_element_type=F32)


def dot_nn(a, b):
    return lax.dot_general(a, b, (((1,), (0,)), ((), ())), preferred_element_type=F32)


def dot_tn(a, b):
    return lax.dot_general(a, b, (((0,), (0,)), ((), ())), preferred_element_type=F32)


def block_probs(hd, b, kv, qg, first, probs, grads):
    at = pl.multiple_of(b * BLOCK, BLOCK)
    q = qg[hd, 0, pl.ds(at, BLOCK), :]
    g = qg[hd, 1, pl.ds(at, BLOCK), :]
    low = first[:, pl.ds(at, BLOCK)] - at
    row = lax.broadcasted_iota(jnp.int32, (BLOCK, BLOCK), 0)
    col = lax.broadcasted_iota(jnp.int32, (BLOCK, BLOCK), 1)
    causal = row <= col

    def rows_of(which, t):
        return kv[which, pl.ds(pl.multiple_of(at + t * BLOCK, BLOCK), BLOCK), :]

    def tiles_of(which, other):
        far = dot_nt(rows_of(which, 0), other)
        near = dot_nt(rows_of(which, 4), other)
        return [jnp.where(causal, near, far)] + [
            dot_nt(rows_of(which, t), other) for t in (1, 2, 3)
        ]

    scores = tiles_of(0, q)
    scores = [
        jnp.where(jnp.where(causal, row + 4 * BLOCK, row) >= low, scores[0], FLOOR)
    ] + [
        jnp.where(row >= low - t * BLOCK, scores[t], FLOOR) for t in (1, 2, 3)
    ]
    peak = functools.reduce(
        jnp.maximum, [jnp.max(s, axis=0, keepdims=True) for s in scores]
    )
    powers = [jnp.exp2((s - peak) * EXP_SCALE) for s in scores]
    total = sum(jnp.sum(e, axis=0, keepdims=True) for e in powers)
    inverse = 1.0 / total
    ps = [e * inverse for e in powers]
    dps = tiles_of(1, g)
    delta = sum(
        jnp.sum(p * d, axis=0, keepdims=True) for p, d in zip(ps, dps)
    )
    dss = [p * (d - delta) for p, d in zip(ps, dps)]
    cols = pl.ds(at, BLOCK)

    def put(ref, values):
        zero = jnp.zeros((BLOCK, BLOCK), F32)
        parts = [jnp.where(causal, zero, values[0])] + values[1:]
        parts = parts + [jnp.where(causal, values[0], zero)]
        for t, part in enumerate(parts):
            rows = pl.ds(pl.multiple_of(at + t * BLOCK, BLOCK), BLOCK)
            ref[rows, cols] = part.astype(BF)

    put(probs, ps)
    put(grads, dss)


def seg_grads(hd, seg, qg, probs, grads):
    rows = pl.ds(pl.multiple_of(seg * HALF, HALF), HALF)
    dk = dot_nn(grads[rows, :], qg[hd, 0])
    dv = dot_nn(probs[rows, :], qg[hd, 1])
    return dk, dv


def block_dq(b, kv, grads):
    at = b * BLOCK
    ds = grads[at : at + 5 * BLOCK, at : at + BLOCK]
    return dot_tn(ds, kv[0, at : at + 5 * BLOCK, :])


def kernel(
    compute,
    q_hbm, k_hbm, v_hbm, g_hbm, doc_hbm,
    dq_out, dk_out, dv_out,
    kv, qg, first, probs, grads, acc, dq_st, st1, r1, st0, r0, st2, docs,
    doc_sem, kv_sem, z_sem, o_sem, qg_sem, snd, snd0, snd_z, snd_o,
    x1_s, x1_r, x0_s, x0_r, odq_s, odq_s0, odq_r, okv_s, okv_s0, odk_r, odv_r,
):
    seq = lax.axis_index("seq")
    tp = lax.axis_index("tp")
    z, x = seq // 4, seq % 4
    y, c = tp // 2, tp % 2
    side = x // 2
    slot = (x % 2) * 8 + tp
    head = x * 4 + y
    up = (((z + 1) % 16) * 4 + x, tp)
    down = (((z + 15) % 16) * 4 + x, tp)
    other = (seq, y * 2 + (1 - c))

    doc_copy = pltpu.make_async_copy(doc_hbm, docs, doc_sem)
    doc_copy.start()

    barrier = pltpu.get_barrier_semaphore()

    def greet(i, carry):
        tx, ty, tc = (x + i // 8) % 4, (y + (i // 2) % 4) % 4, (c + i % 2) % 2
        pl.semaphore_signal(
            barrier, inc=1, device_id=(z * 4 + tx, ty * 2 + tc), device_id_type=MESH
        )
        return carry

    lax.fori_loop(1, 32, greet, 0)
    for peer in (up, down):
        pl.semaphore_signal(barrier, inc=1, device_id=peer, device_id_type=MESH)
    pl.semaphore_wait(barrier, 33)

    def key_rows(at):
        return pl.ds(pl.multiple_of(at, ROWS), ROWS)

    def in_pairs(h):
        kcols = pl.ds(pl.multiple_of(h * HEAD, HEAD), HEAD)
        pairs = [
            (k_hbm.at[:, kcols], kv.at[0, key_rows(WINDOW + ROWS * slot), :], kv_sem.at[slot]),
            (v_hbm.at[:, kcols], kv.at[1, key_rows(WINDOW + ROWS * slot), :], kv_sem.at[slot]),
        ]
        for hd in range(2):
            qcols = pl.ds(pl.multiple_of(h * 2 * HEAD + hd * HEAD, HEAD), HEAD)
            for j, ref in enumerate((q_hbm, g_hbm)):
                pairs.append(
                    (ref.at[:, qcols], qg.at[hd, j, key_rows(ROWS * slot), :], qg_sem.at[hd])
                )
        return pairs

    def remote(src, dst, send, recv, dev):
        pltpu.make_async_remote_copy(
            src_ref=src, dst_ref=dst, send_sem=send, recv_sem=recv,
            device_id=dev, device_id_type=MESH,
        ).start()

    def send_in(kinds):
        @pl.when(c == side)
        def _():
            for src, dst, sem in in_pairs(head)[kinds]:
                pltpu.make_async_copy(src, dst, sem).start()

        @pl.when(c != side)
        def _():
            for src, dst, sem in in_pairs(head)[kinds]:
                remote(src, dst, snd0, sem, (seq, y * 2 + side))

        def step(i, carry):
            tx = (x + i % 4) % 4
            ty = (y + i % 4 + i // 4) % 4
            for src, dst, sem in in_pairs(tx * 4 + ty)[kinds]:
                remote(src, dst, snd, sem, (z * 4 + tx, ty * 2 + side))
            return carry

        lax.fori_loop(1, 16, step, 0)

    send_in(slice(0, 2))
    send_in(slice(2, 4))
    send_in(slice(4, 6))

    def bytes_of(ref, sem):
        return pltpu.make_async_copy(ref, ref, sem)

    doc_copy.wait()
    base = z * 1024 + c * HALF - WINDOW
    pos = lax.broadcasted_iota(jnp.int32, (1, HALF), 1) + (base + WINDOW)
    low = jnp.zeros((1, HALF), jnp.int32)
    start = jnp.int32(0)
    for d in range(DOCS):
        low = jnp.where(pos >= start, start, low)
        start = start + docs[d]
    first[...] = low - base

    zero = jnp.zeros((BLOCK, BLOCK), BF)
    for ref in (probs, grads):
        ref[0:BLOCK, BLOCK : 2 * BLOCK] = zero
        ref[SPAN - BLOCK : SPAN, 0:BLOCK] = zero

    def relay(s, carry):
        mine = kv.at[:, key_rows(WINDOW + ROWS * s), :]
        bytes_of(mine, kv_sem.at[s]).wait()
        remote(mine, kv.at[:, key_rows(ROWS * s), :], snd_z, z_sem.at[s], up)

        @pl.when(c == 0)
        def _():
            remote(mine, kv.at[:, key_rows(HALF + ROWS * s), :], snd_o, o_sem, other)

        return carry

    lax.fori_loop(0, 16, relay, 0)

    def relay_core(s, carry):
        mine = kv.at[:, key_rows(ROWS * s), :]
        bytes_of(mine, z_sem.at[s]).wait()

        @pl.when(c == 1)
        def _():
            remote(mine, kv.at[:, key_rows(HALF + ROWS * s), :], snd_o, o_sem, other)

        return carry

    lax.fori_loop(0, 16, relay_core, 0)
    bytes_of(kv.at[:, HALF:WINDOW, :], o_sem).wait()

    def owner(i):
        s = (slot + i) % 16
        return s, (z * 4 + 2 * c + s // 8, s % 8)

    def send_out(i, pairs_of, sem0, sem):
        pass

    def out_dq(hd):
        cols = pl.ds(pl.multiple_of(head * 2 * HEAD + hd * HEAD, HEAD), HEAD)
        dst = dq_out.at[:, cols]

        def src(s):
            return dq_st.at[hd, key_rows(ROWS * s), :]

        @pl.when(c == side)
        def _():
            pltpu.make_async_copy(src(slot), dst, odq_r).start()

        @pl.when(c != side)
        def _():
            s, dev = owner(0)
            remote(src(s), dst, odq_s0, odq_r, dev)

        def step(i, carry):
            s, dev = owner(i)
            remote(src(s), dst, odq_s, odq_r, dev)
            return carry

        lax.fori_loop(1, 16, step, 0)

    def do_dq(hd):
        if compute:
            for b in range(2):
                dq_st[hd, b * BLOCK : (b + 1) * BLOCK, :] = (
                    block_dq(b, kv, grads) * SCALE
                ).astype(BF)
        else:
            dq_st[hd] = qg[hd, 0]
        out_dq(hd)

    def do_probs(hd):
        bytes_of(qg.at[hd], qg_sem.at[hd]).wait()
        if compute:

            def one(b, carry):
                block_probs(hd, b, kv, qg, first, probs, grads)
                return carry

            lax.fori_loop(0, 2, one, 0)

    def grads_of(hd, seg):
        if compute:
            return seg_grads(hd, seg, qg, probs, grads)
        return qg[hd, 0].astype(F32), qg[hd, 1].astype(F32)

    def seg_rows(seg):
        return pl.ds(pl.multiple_of(seg * HALF, HALF), HALF)

    do_probs(0)

    def first_head(seg, carry):
        dk, dv = grads_of(0, seg)
        acc[0, seg_rows(seg), :] = dk
        acc[1, seg_rows(seg), :] = dv
        return carry

    lax.fori_loop(0, 3, first_head, 0)
    do_dq(0)
    do_probs(1)

    def add_up(seg):
        dk, dv = grads_of(1, seg)
        acc[0, seg_rows(seg), :] += dk
        acc[1, seg_rows(seg), :] += dv

    def ship_middle():
        st1[...] = acc[:, HALF:WINDOW, :].astype(BF)
        remote(st1, r1, x1_s, x1_r, other)

    @pl.when(c == 0)
    def _():
        add_up(1)
        ship_middle()
        add_up(0)
        st0[...] = acc[:, 0:HALF, :].astype(BF)

    @pl.when(c == 1)
    def _():
        add_up(0)
        add_up(1)
        ship_middle()

    CH = 4
    CR = HALF // CH

    @pl.when(c == 1)
    def _():
        bytes_of(r1, x1_r).wait()
        st0[...] = (acc[:, 0:HALF, :] + r1[...].astype(F32)).astype(BF)

    for ch in range(CH):
        remote(
            st0.at[:, ch * CR : (ch + 1) * CR, :], r0.at[:, ch * CR : (ch + 1) * CR, :],
            x0_s, x0_r.at[ch], down,
        )
    add_up(2)
    do_dq(1)

    @pl.when(c == 0)
    def _():
        bytes_of(r1, x1_r).wait()
        acc[:, WINDOW:SPAN, :] += r1[...].astype(F32)

    kcols = pl.ds(pl.multiple_of(head * HEAD, HEAD), HEAD)

    def out_pairs(s):
        return (
            (st2.at[0, key_rows(ROWS * s), :], dk_out.at[:, kcols], odk_r),
            (st2.at[1, key_rows(ROWS * s), :], dv_out.at[:, kcols], odv_r),
        )

    def finish(ch, carry):
        rows = pl.ds(pl.multiple_of(ch * CR, CR), CR)
        bytes_of(r0.at[:, rows, :], x0_r.at[ch]).wait()
        late = pl.ds(pl.multiple_of(WINDOW + ch * CR, CR), CR)
        whole = acc[:, late, :] + r0[:, rows, :].astype(F32)
        st2[0, rows, :] = (whole[0] * SCALE).astype(BF)
        st2[1, rows, :] = whole[1].astype(BF)

        def step(j, inner):
            s = ch * 4 + j
            dev = (z * 4 + 2 * c + s // 8, s % 8)
            here = (s == slot) & (c == side)

            @pl.when(here)
            def _():
                for src, dst, sem in out_pairs(s):
                    pltpu.make_async_copy(src, dst, sem).start()

            @pl.when(jnp.logical_not(here))
            def _():
                for src, dst, sem in out_pairs(s):
                    remote(src, dst, okv_s, sem, dev)

            return inner

        return lax.fori_loop(0, 4, step, carry)

    lax.fori_loop(0, CH, finish, 0)

    bytes_of(kv.at[:, 0:1440, :], snd).wait()

    @pl.when(c != side)
    def _():
        bytes_of(kv.at[:, 0:96, :], snd0).wait()
        bytes_of(dq_st.at[:, 0:ROWS, :], odq_s0).wait()
        bytes_of(st2, okv_s).wait()

    @pl.when(c == side)
    def _():
        bytes_of(st2.at[:, 0 : HALF - ROWS, :], okv_s).wait()

    bytes_of(kv.at[:, 0:HALF, :], snd_z).wait()
    bytes_of(kv.at[:, 0:HALF, :], snd_o).wait()
    bytes_of(st1, x1_s).wait()
    bytes_of(st0, x0_s).wait()
    bytes_of(dq_st.at[:, 0 : HALF - ROWS, :], odq_s).wait()
    bytes_of(dq_out, odq_r).wait()
    bytes_of(dk_out, odk_r).wait()
    bytes_of(dv_out, odv_r).wait()


def per_device(compute, queries, key_states, value_state_rows, out_grad, doc_lengths):
    any_space = pl.BlockSpec(memory_space=pl.ANY)
    dma = pltpu.SemaphoreType.DMA
    return pl.pallas_call(
        functools.partial(kernel, compute),
        out_shape=(
            jax.ShapeDtypeStruct(queries.shape, BF),
            jax.ShapeDtypeStruct(key_states.shape, BF),
            jax.ShapeDtypeStruct(value_state_rows.shape, BF),
        ),
        in_specs=[any_space] * 5,
        out_specs=(any_space,) * 3,
        scratch_shapes=[
            pltpu.VMEM((2, SPAN, HEAD), BF),
            pltpu.VMEM((2, 2, HALF, HEAD), BF),
            pltpu.VMEM((1, HALF), jnp.int32),
            pltpu.VMEM((SPAN, HALF), BF),
            pltpu.VMEM((SPAN, HALF), BF),
            pltpu.VMEM((2, SPAN, HEAD), F32),
            pltpu.VMEM((2, HALF, HEAD), BF),
            pltpu.VMEM((2, HALF, HEAD), BF),
            pltpu.VMEM((2, HALF, HEAD), BF),
            pltpu.VMEM((2, HALF, HEAD), BF),
            pltpu.VMEM((2, HALF, HEAD), BF),
            pltpu.VMEM((2, HALF, HEAD), BF),
            pltpu.SMEM((DOCS,), jnp.int32),
            dma, dma((16,)), dma((16,)), dma, dma((2,)), dma, dma, dma, dma,
            dma, dma, dma, dma((4,)), dma, dma, dma, dma, dma, dma, dma,
        ],
        compiler_params=pltpu.CompilerParams(
            collective_id=0, has_side_effects=True, vmem_limit_bytes=60 * 1024 * 1024
        ),
        name="window_attention_backward",
    )(queries, key_states, value_state_rows, out_grad, doc_lengths)


COMPUTE = True


def solution(mesh):
    rows = P(("seq", "tp"), None)
    return jax.shard_map(
        functools.partial(per_device, COMPUTE),
        mesh=mesh,
        in_specs=(rows, rows, rows, rows, P()),
        out_specs=(rows, rows, rows),
        check_vma=False,
    )
```

time: 179 us -> 49.9 us (0.28)
  starting transfers between devices: 49.4 us -> 0 us
  waiting for transfers between devices: 46.3 us -> 0 us
  Pallas kernels: 0 us -> 45.7 us
  local copies, waits for them, and re-layouts: 36.7 us -> 3.31 us
  matrix products: 22.8 us -> 0 us
  other arithmetic: 10.7 us -> 0 us
  blocking collectives: 10 us -> 0 us
    pallas_call x0 -> x1, Pallas kernels: none -> 45.7 us  [per_device(): pl.pallas_call(functools.partial(kernel, compute), out_shape=(jax.ShapeDt...]
    all_to_all x6 -> x0, starting transfers between devices: 33 us -> none  [the longest x1 10.2 us: per_device(): lax.all_to_all(key_states, 'tp', split_axis=1, concat_axis=0, tiled=True)]
    ppermute x8 -> x0, waiting for transfers between devices: 28.7 us -> none  [passed_along(): lax.ppermute(value, axis, [(source, source + steps) for source in range(i...]
    dot_general x30 -> x0, matrix products: 22.8 us -> none  [the longest x5 8.5 us: output_work(): jnp.einsum('grqk,kgd->qgrd', probs_bf, value_tile, preferred_element_type...]
    all_to_all x6 -> x0, waiting for transfers between devices: 17.6 us -> none  [the longest x1 5.7 us: per_device(): lax.all_to_all(out_grad, 'tp', split_axis=1, concat_axis=0, tiled=True)]
    ppermute x8 -> x0, starting transfers between devices: 16.4 us -> none  [passed_along(): lax.ppermute(value, axis, [(source, source + steps) for source in range(i...]
    slice x13 -> x0, local copies, waits for them, and re-layouts: 11.8 us -> none  [the longest x8 8.73 us: split_pair(): pair[1].reshape(stretch_rows, kv_local, HEAD_SIZE)]
    all_to_all x1 -> x0, blocking collectives: 10 us -> none  [per_device(): lax.all_to_all(key_gradient, 'tp', split_axis=0, concat_axis=1, tiled=True)]
  transfers between devices with their start and end apart: 14 -> 0, of which waited for: 7 -> 0; matrix products, arithmetic and copies ran while one was open for 14% -> 0% of each run, Pallas kernels for 0% -> 0%
where the time goes in v1:
time: 49.9 us; the launch traced here: 49.7 us
  Pallas kernels  45.7 us (92%)
  local copies, waits for them, and re-layouts  3.31 us (7%)
  between operations  0.65 us (1%)
    pallas_call x1, Pallas kernels, per_device(): pl.pallas_call(functools.partial(kernel, compute), out_shape=(jax.ShapeDt...  45.7 us
    unnamed x7, local copies, waits for them, and re-layouts  3.31 us

profile of v1, /device:TPU:1, one launch (start us, length us, event | category | flops | bytes accessed | tf_op | source)
XLA Modules:
  0.0 49.7 jit_solution(8754413925376598990)
XLA Ops:
  0.6 45.7 %window_attention_backward.1 = (bf16[32,4096]{1,0:T(8,128)(2,1)}, bf16[32,2048]{1,0:T(8,128)(2,1)}, bf16[32,2048]{1,0:T(8,128)(2,1)}) custom-call(bf16[32,4096]{1,0:T(8,128)(2,1)} %q_hbm.1, bf16[32,2048]{1,0:T(8,128)(2,1)} %k_hbm.1, bf16[32,2048]{1,0:T(8,128)(2,1)} %v_hbm.1, bf16[32,4096]{1,0:T(8,128)(2,1)} %g_hbm.1, s32[16]{0:T(128)} %doc_hbm.1), custom_call_target="tpu_custom_call" | custom-call | tf_op jit(solution)/shard_map/window_attention_backward/pallas_call | solution.py:404
  46.4 0.0 copy-start.1
  46.4 1.7 %copy.11 = bf16[32,4096]{1,0:T(8,128)(2,1)} copy(bf16[32,4096]{1,0:T(8,128)(2,1)} %get-tuple-element.6) | data formatting | bytes 524288
  48.1 0.0 copy-done.1
  48.1 0.0 copy-start
  48.1 0.7 %copy.12 = bf16[32,2048]{1,0:T(8,128)(2,1)} copy(bf16[32,2048]{1,0:T(8,128)(2,1)S(1)} %copy-done.1) | data formatting | bytes 262144
  48.8 0.3 copy-done
  49.0 0.7 %copy.13 = bf16[32,2048]{1,0:T(8,128)(2,1)} copy(bf16[32,2048]{1,0:T(8,128)(2,1)S(1)} %copy-done) | data formatting | bytes 262144
Async XLA Ops:
  46.4 1.7 %copy-start.1 = (bf16[32,2048]{1,0:T(8,128)(2,1)S(1)}, bf16[32,2048]{1,0:T(8,128)(2,1)}, u32[]{:S(2)}) copy-start(bf16[32,2048]{1,0:T(8,128)(2,1)} %get-tuple-element.7) | copy-start | bytes 393220
  48.1 1.0 %copy-start = (bf16[32,2048]{1,0:T(8,128)(2,1)S(1)}, bf16[32,2048]{1,0:T(8,128)(2,1)}, u32[]{:S(2)}) copy-start(bf16[32,2048]{1,0:T(8,128)(2,1)} %get-tuple-element.8) | copy-start | bytes 393220

commit v2 on v0

v2 whole, which is shorter than its diff:
```python
import functools
import math

import jax
import jax.numpy as jnp
from jax import lax
from jax.experimental import pallas as pl
from jax.experimental.pallas import tpu as pltpu
from jax.sharding import PartitionSpec as P

MESH = pl.DeviceIdType.MESH
HEAD = 128
ROWS = 32
HALF = 512
BLOCK = 256
SPAN = 3 * HALF
WINDOW = 1024
DOCS = 16
PLANES = 16
SCALE = 168.0 ** (-0.5)
EXP_SCALE = SCALE / math.log(2.0)
FLOOR = -1e30
BF = jnp.bfloat16
F32 = jnp.float32


def dot_nt(a, b):
    return lax.dot_general(a, b, (((1,), (1,)), ((), ())), preferred_element_type=F32)


def dot_nn(a, b):
    return lax.dot_general(a, b, (((1,), (0,)), ((), ())), preferred_element_type=F32)


def dot_tn(a, b):
    return lax.dot_general(a, b, (((0,), (0,)), ((), ())), preferred_element_type=F32)


def unit(hd, j, at, kv, qg, first, acc, dq):
    qrows = pl.ds(pl.multiple_of(j * BLOCK, BLOCK), BLOCK)
    q = qg[hd, 0, qrows, :]
    g = qg[hd, 1, qrows, :]
    low = first[:, qrows] - at
    row = lax.broadcasted_iota(jnp.int32, (BLOCK, BLOCK), 0)
    col = lax.broadcasted_iota(jnp.int32, (BLOCK, BLOCK), 1)
    causal = row <= col
    def rows_at(t):
        return pl.ds(pl.multiple_of(at + t * BLOCK, BLOCK), BLOCK)
    def tiles_of(which, w):
        far = dot_nt(kv[which, rows_at(0), :], w)
        near = dot_nt(kv[which, rows_at(4), :], w)
        return [jnp.where(causal, near, far)] + [dot_nt(kv[which, rows_at(t), :], w) for t in (1, 2, 3)]
    scores = tiles_of(0, q)
    scores = [jnp.where(jnp.where(causal, row + 4 * BLOCK, row) >= low, scores[0], FLOOR)] + [
        jnp.where(row >= low - t * BLOCK, scores[t], FLOOR) for t in (1, 2, 3)]
    peak = functools.reduce(jnp.maximum, scores)
    peak = jnp.max(peak, axis=0, keepdims=True) * EXP_SCALE
    ps = [jnp.exp2(s * EXP_SCALE - peak) for s in scores]
    total = jnp.sum(functools.reduce(jnp.add, ps), axis=0, keepdims=True)
    inverse = 1.0 / total
    dps = tiles_of(1, g)
    ps = [p * inverse for p in ps]
    ts = [p * d for p, d in zip(ps, dps)]
    delta = jnp.sum(functools.reduce(jnp.add, ts), axis=0, keepdims=True)
    dss = [t - p * delta for p, t in zip(ps, ts)]
    zero = jnp.zeros((BLOCK, BLOCK), F32)
    def spread(v):
        parts = [jnp.where(causal, zero, v[0])] + v[1:] + [jnp.where(causal, v[0], zero)]
        return [p.astype(BF) for p in parts]
    pb = spread(ps); db = spread(dss)
    for t in range(5):
        acc[1, rows_at(t), :] += dot_nn(pb[t], g)
        acc[0, rows_at(t), :] += dot_nn(db[t], q)
    out = functools.reduce(
        jnp.add, [dot_tn(db[t], kv[0, rows_at(t), :]) for t in range(5)]
    )
    cols = pl.ds(pl.multiple_of(hd * HEAD, HEAD), HEAD)
    dq[qrows, cols] = (out * SCALE).astype(BF)


VLIM = 64800
PUT = True
OUT_SHAPE = pltpu.VMEM


def OUT_SPEC():
    return pl.BlockSpec(memory_space=pltpu.VMEM)


def PUT_SPEC():
    return pl.BlockSpec(memory_space=pltpu.VMEM)


def kernel(
    q_hbm, k_hbm, v_hbm, g_hbm, doc_hbm,
    dq_out, dk_out, dv_out,
    kv, qg, first, acc, dq_st, st1, r1, st0, r0, st2, docs,
    doc_sem, kv_sem, z_sem, o_sem, qg_sem, snd, snd0, snd_z, snd_o, snd_o2,
    x1_s, x1_r, x0_s, x0_r, odq_s, odq_r, okv_s, odk_r, odv_r,
):
    seq = lax.axis_index("seq")
    tp = lax.axis_index("tp")
    z, x = seq // 4, seq % 4
    y, c = tp // 2, tp % 2
    side = x % 2
    slot = (x // 2) * 8 + tp
    head = x * 4 + y
    first_plane, last_plane = z == 0, z == PLANES - 1
    up = (((z + 1) % PLANES) * 4 + x, tp)
    down = (((z + PLANES - 1) % PLANES) * 4 + x, tp)
    other = (seq, y * 2 + (1 - c))

    doc_copy = pltpu.make_async_copy(doc_hbm, docs, doc_sem)
    doc_copy.start()

    barrier = pltpu.get_barrier_semaphore()
    xs = [(x + d) % 4 for d in range(4)]
    ys = [(y + d) % 4 for d in range(4)]
    for dx, dy in sorted(
        ((a, b) for a in range(4) for b in range(4)),
        key=lambda p: -(min(p[0], 4 - p[0]) + min(p[1], 4 - p[1])),
    ):
        for tc in (1 - c, c) if (dx, dy) != (0, 0) else (1 - c,):
            pl.semaphore_signal(
                barrier, inc=1, device_id=(z * 4 + xs[dx], ys[dy] * 2 + tc),
                device_id_type=MESH,
            )

    @pl.when(z < PLANES - 1)
    def _():
        pl.semaphore_signal(barrier, inc=1, device_id=up, device_id_type=MESH)

    @pl.when(z > 0)
    def _():
        pl.semaphore_signal(barrier, inc=1, device_id=down, device_id_type=MESH)

    acc[...] = jnp.zeros(acc.shape, F32)

    @pl.when(first_plane)
    def _():
        kv[:, 0:WINDOW, :] = jnp.zeros((2, WINDOW, HEAD), BF)

    @pl.when(last_plane)
    def _():
        r0[...] = jnp.zeros(r0.shape, BF)

    pl.semaphore_wait(barrier, 33 - z // (PLANES - 1) - (PLANES - 1 - z) // (PLANES - 1))

    def key_rows(at):
        return pl.ds(pl.multiple_of(at, ROWS), ROWS)

    def remote(src, dst, send, recv, dev):
        pltpu.make_async_remote_copy(
            src_ref=src, dst_ref=dst, send_sem=send, recv_sem=recv,
            device_id=dev, device_id_type=MESH,
        ).start()

    def bytes_of(ref, sem):
        return pltpu.make_async_copy(ref, ref, sem)

    my_keys = key_rows(WINDOW + x * BLOCK + ROWS * tp)
    my_rows = key_rows(ROWS * slot)

    def in_pairs(h):
        kcols = pl.ds(pl.multiple_of(h * HEAD, HEAD), HEAD)
        pairs = [
            (k_hbm.at[:, kcols], kv.at[0, my_keys, :], kv_sem.at[slot]),
            (v_hbm.at[:, kcols], kv.at[1, my_keys, :], kv_sem.at[slot]),
        ]
        for hd in range(2):
            qcols = pl.ds(pl.multiple_of(h * 2 * HEAD + hd * HEAD, HEAD), HEAD)
            for j, ref in enumerate((q_hbm, g_hbm)):
                pairs.append((ref.at[:, qcols], qg.at[hd, j, my_rows, :], qg_sem.at[hd]))
        return pairs

    def send_here(kinds):
        @pl.when(c == side)
        def _():
            for src, dst, sem in in_pairs(head)[kinds]:
                pltpu.make_async_copy(src, dst, sem).start()

        @pl.when(c != side)
        def _():
            for src, dst, sem in in_pairs(head)[kinds]:
                remote(src, dst, snd0, sem, other)

    def send_away(kinds, i):
        tx = (x + i % 4) % 4
        ty = (y + i % 4 + i // 4) % 4
        for src, dst, sem in in_pairs(tx * 4 + ty)[kinds]:
            remote(src, dst, snd, sem, (z * 4 + tx, ty * 2 + side))

    KEYS, HEAD0, HEAD1 = slice(0, 2), slice(2, 4), slice(4, 6)

    def send_all(kinds):
        def step(i, carry):
            send_away(kinds, i)
            return carry

        lax.fori_loop(1, 16, step, 0)

    send_all(KEYS)
    send_here(KEYS)
    send_all(HEAD0)
    send_here(HEAD0)
    send_here(HEAD1)

    doc_copy.wait()
    for j in range(2):
        begin = z * 1024 + (2 * j + c) * BLOCK
        pos = lax.broadcasted_iota(jnp.int32, (1, BLOCK), 1) + begin
        low = jnp.zeros((1, BLOCK), jnp.int32)
        start = jnp.int32(0)
        for d in range(DOCS):
            low = jnp.where(pos >= start, start, low)
            start = start + docs[d]
        first[:, j * BLOCK : (j + 1) * BLOCK] = low - (z - 1) * 1024

    def relay(s):
        mine = kv.at[:, key_rows(WINDOW + (2 * (s // 8) + c) * BLOCK + ROWS * (s % 8)), :]
        ahead = kv.at[:, key_rows((2 * (s // 8) + c) * BLOCK + ROWS * (s % 8)), :]
        bytes_of(mine, kv_sem.at[s]).wait()

        @pl.when(z < PLANES - 1)
        def _():
            remote(mine, ahead, snd_z, z_sem.at[s], up)

        remote(mine, mine, snd_o, o_sem, other)

    relay(0)

    def relay_send(s, carry):
        relay(s)
        send_away(HEAD1, s)
        return carry

    lax.fori_loop(1, 16, relay_send, 0)

    def relay_core(s, carry):
        mine = kv.at[:, key_rows((2 * (s // 8) + c) * BLOCK + ROWS * (s % 8)), :]
        bytes_of(mine, z_sem.at[s]).wait()
        remote(mine, mine, snd_o2, o_sem, other)
        return carry

    @pl.when(z > 0)
    def _():
        lax.fori_loop(0, 16, relay_core, 0)
        bytes_of(kv.at[:, 0:WINDOW, :], o_sem).wait()

    @pl.when(first_plane)
    def _():
        bytes_of(kv.at[:, 0:HALF, :], o_sem).wait()

    def run_unit(hd, j):
        at = pl.multiple_of((2 * j + c) * BLOCK, BLOCK)
        if COMPUTE:
            unit(hd, j, at, kv, qg, first, acc, dq_st)

    def first_head(j, carry):
        run_unit(0, j)
        return carry

    def tile(t):
        return acc[:, pl.ds(pl.multiple_of(t * BLOCK, BLOCK), BLOCK), :]

    def ship_core(m, t):
        st1[m] = tile(t).astype(BF)
        remote(st1.at[m], r1.at[m], x1_s, x1_r.at[m], other)

    def ship_down(i, total):
        st0[i] = total.astype(BF)

        @pl.when(z > 0)
        def _():
            for h in range(2):
                part = slice(h * 128, (h + 1) * 128)
                remote(
                    st0.at[i, :, part, :], r0.at[i, :, part, :],
                    x0_s, x0_r.at[2 * i + h], down,
                )

    bytes_of(qg.at[0], qg_sem.at[0]).wait()
    lax.fori_loop(0, 2, first_head, 0)
    bytes_of(qg.at[1], qg_sem.at[1]).wait()
    run_unit(1, 0)

    ship_core(0, 1 + c)

    @pl.when(c == 0)
    def _():
        ship_down(0, tile(0))

    @pl.when(c == 1)
    def _():
        bytes_of(r1.at[0], x1_r.at[0]).wait()
        ship_down(0, tile(1) + r1[0].astype(F32))

    run_unit(1, 1)

    ship_core(1, 3 + c)

    @pl.when(c == 0)
    def _():
        bytes_of(r1.at[0], x1_r.at[0]).wait()
        ship_down(1, tile(2) + r1[0].astype(F32))

    ship_core(2, 5 + c)
    bytes_of(r1.at[1], x1_r.at[1]).wait()

    @pl.when(c == 1)
    def _():
        ship_down(1, tile(3) + r1[1].astype(F32))

    own = c == side

    def send_out(s, pairs, sem0):
        dev = (z * 4 + 2 * (s // 8) + c, s % 8)
        here = own & (s == slot)

        @pl.when(here)
        def _():
            for src, dst, sem in pairs:
                pltpu.make_async_copy(src, dst, sem).start()

        @pl.when(jnp.logical_not(here))
        def _():
            for src, dst, sem in pairs:
                remote(src, dst, sem0, sem, dev)

    qcols = pl.ds(pl.multiple_of(head * 2 * HEAD, 2 * HEAD), 2 * HEAD)
    kcols = pl.ds(pl.multiple_of(head * HEAD, HEAD), HEAD)

    def dq_step(i, carry):
        s = (slot + i) % 16
        send_out(s, [(dq_st.at[key_rows(ROWS * s), :], dq_out.at[:, qcols], odq_r)], odq_s)
        return carry

    lax.fori_loop(0, 16, dq_step, 0)

    def finish(j, rows, extra):
        at = pl.ds(pl.multiple_of(WINDOW + (2 * j + c) * BLOCK + rows.start, 128), rows.stop - rows.start)
        whole = acc[:, at, :] + r0[j, :, rows, :].astype(F32)
        if extra is not None:
            whole = whole + extra[:, rows, :].astype(F32)
        here = slice(j * BLOCK + rows.start, j * BLOCK + rows.stop)
        st2[0, here, :] = (whole[0] * SCALE).astype(BF)
        st2[1, here, :] = whole[1].astype(BF)

        def step(i, carry):
            s = j * 8 + rows.start // ROWS + i
            send_out(
                s,
                [
                    (st2.at[0, key_rows(ROWS * s), :], dk_out.at[:, kcols], odk_r),
                    (st2.at[1, key_rows(ROWS * s), :], dv_out.at[:, kcols], odv_r),
                ],
                okv_s,
            )
            return carry

        lax.fori_loop(0, (rows.stop - rows.start) // ROWS, step, 0)

    bytes_of(r1.at[2], x1_r.at[2]).wait()
    def await_down(i, h):
        @pl.when(z < PLANES - 1)
        def _():
            bytes_of(r0.at[i, :, h * 128 : (h + 1) * 128, :], x0_r.at[2 * i + h]).wait()

    await_down(0, 0)
    await_down(0, 1)
    finish(0, slice(0, BLOCK), r1.at[1 + c])

    @pl.when(c == 0)
    def _():
        acc[:, WINDOW + 2 * BLOCK : WINDOW + 3 * BLOCK, :] += r1[2].astype(F32)

    for h in range(2):
        rows = slice(h * 128, (h + 1) * 128)
        await_down(1, h)
        finish(1, rows, None)

    bytes_of(kv.at[:, 0:1440, :], snd).wait()

    @pl.when(jnp.logical_not(own))
    def _():
        bytes_of(kv.at[:, 0:96, :], snd0).wait()
        bytes_of(dq_st, odq_s).wait()
        bytes_of(st2, okv_s).wait()

    @pl.when(own)
    def _():
        bytes_of(dq_st.at[0 : HALF - ROWS, :], odq_s).wait()
        bytes_of(st2.at[:, 0 : HALF - ROWS, :], okv_s).wait()

    bytes_of(kv.at[:, 0:HALF, :], snd_o).wait()
    bytes_of(st1, x1_s).wait()

    @pl.when(z < PLANES - 1)
    def _():
        bytes_of(kv.at[:, 0:HALF, :], snd_z).wait()

    @pl.when(z > 0)
    def _():
        bytes_of(kv.at[:, 0:HALF, :], snd_o2).wait()
        bytes_of(st0, x0_s).wait()
    bytes_of(dq_out, odq_r).wait()
    bytes_of(dk_out, odk_r).wait()
    bytes_of(dv_out, odv_r).wait()


def put_kernel(a, b, d, oa, ob, od, sem):
    copies = [
        pltpu.make_async_copy(src, dst, sem.at[i])
        for i, (src, dst) in enumerate(((a, oa), (b, ob), (d, od)))
    ]
    for copy in copies:
        copy.start()
    for copy in copies:
        copy.wait()


def per_device(queries, key_states, value_state_rows, out_grad, doc_lengths):
    any_space = pl.BlockSpec(memory_space=pl.ANY)
    vmem_space = pl.BlockSpec(memory_space=pltpu.VMEM)
    dma = pltpu.SemaphoreType.DMA
    shapes = [queries.shape, key_states.shape, value_state_rows.shape]
    results = pl.pallas_call(
        kernel,
        out_shape=tuple(OUT_SHAPE(s, BF) for s in shapes),
        in_specs=[pl.BlockSpec(memory_space=pltpu.HBM)] * 5,
        out_specs=(OUT_SPEC(),) * 3,
        scratch_shapes=[
            pltpu.VMEM((2, 2 * WINDOW, HEAD), BF),
            pltpu.VMEM((2, 2, HALF, HEAD), BF),
            pltpu.VMEM((1, HALF), jnp.int32),
            pltpu.VMEM((2, 2 * WINDOW, HEAD), F32),
            pltpu.VMEM((HALF, 2 * HEAD), BF),
            pltpu.VMEM((3, 2, BLOCK, HEAD), BF),
            pltpu.VMEM((3, 2, BLOCK, HEAD), BF),
            pltpu.VMEM((2, 2, BLOCK, HEAD), BF),
            pltpu.VMEM((2, 2, BLOCK, HEAD), BF),
            pltpu.VMEM((2, HALF, HEAD), BF),
            pltpu.SMEM((DOCS,), jnp.int32),
            dma, dma((16,)), dma((16,)), dma, dma((2,)), dma, dma, dma, dma, dma,
            dma, dma((3,)), dma, dma((4,)), dma, dma, dma, dma, dma,
        ],
        compiler_params=pltpu.CompilerParams(
            collective_id=0, has_side_effects=True, vmem_limit_bytes=VLIM * 1024
        ),
        name="window_attention_backward",
    )(queries, key_states, value_state_rows, out_grad, doc_lengths)
    if not PUT:
        return results
    return pl.pallas_call(
        put_kernel,
        out_shape=tuple(jax.ShapeDtypeStruct(s, BF) for s in shapes),
        in_specs=[PUT_SPEC()] * 3,
        out_specs=(any_space,) * 3,
        scratch_shapes=[dma((3,))],
        compiler_params=pltpu.CompilerParams(vmem_limit_bytes=1024 * 1024),
        name="put_results",
    )(*results)


COMPUTE = True


def solution(mesh):
    rows = P(("seq", "tp"), None)
    return jax.shard_map(
        per_device,
        mesh=mesh,
        in_specs=(rows, rows, rows, rows, P()),
        out_specs=(rows, rows, rows),
        check_vma=False,
    )
```

time: 179 us -> 40.7 us (0.23)
  the two profiles are of different devices: /device:TPU:1 before, /device:TPU:385 now
where the time goes in v2:
time: 40.7 us; the launch traced here: 40.5 us
  Pallas kernels  39.9 us (98%)
  between operations  0.64 us (2%)
    pallas_call x1, Pallas kernels, per_device(): pl.pallas_call(kernel, out_shape=tuple((OUT_SHAPE(s, BF) for s in shapes)...  39.1 us

profile of v2, /device:TPU:385, one launch (start us, length us, event | category | flops | bytes accessed | tf_op | source)
XLA Modules:
  0.0 40.5 jit_solution(13132804660191611353)
XLA Ops:
  0.6 39.1 %window_attention_backward.1 = (bf16[32,4096]{1,0:T(8,128)(2,1)S(1)}, bf16[32,2048]{1,0:T(8,128)(2,1)S(1)}, bf16[32,2048]{1,0:T(8,128)(2,1)S(1)}) custom-call(bf16[32,4096]{1,0:T(8,128)(2,1)} %q_hbm.1, bf16[32,2048]{1,0:T(8,128)(2,1)} %k_hbm.1, bf16[32,2048]{1,0:T(8,128)(2,1)} %v_hbm.1, bf16[32,4096]{1,0:T(8,128)(2,1)} %g_hbm.1, s32[16]{0:T(128)} %doc_hbm.1), custom_call_target="tpu_custom_call" | custom-call | tf_op jit(solution)/shard_map/window_attention_backward/pallas_call | solution.py:427
  39.7 0.8 %put_results.1 = (bf16[32,4096]{1,0:T(8,128)(2,1)}, bf16[32,2048]{1,0:T(8,128)(2,1)}, bf16[32,2048]{1,0:T(8,128)(2,1)}) custom-call(bf16[32,4096]{1,0:T(8,128)(2,1)S(1)} %get-tuple-element.6.a, bf16[32,2048]{1,0:T(8,128)(2,1)S(1)} %get-tuple-element.7.b, bf16[32,2048]{1,0:T(8,128)(2,1)S(1)} %get-tuple-element.8.d), custom_call_target="tpu_custom_call" | custom-call | tf_op jit(solution)/shard_map/put_results/pallas_call | solution.py:454

commit v3 on v2

--- a/solution.py
+++ b/solution.py
@@ -199,10 +199,10 @@
 
         lax.fori_loop(1, 16, step, 0)
 
+    send_here(KEYS)
     send_all(KEYS)
-    send_here(KEYS)
+    send_here(HEAD0)
     send_all(HEAD0)
-    send_here(HEAD0)
     send_here(HEAD1)
 
     doc_copy.wait()
@@ -216,9 +216,16 @@
             start = start + docs[d]
         first[:, j * BLOCK : (j + 1) * BLOCK] = low - (z - 1) * 1024
 
-    def relay(s):
-        mine = kv.at[:, key_rows(WINDOW + (2 * (s // 8) + c) * BLOCK + ROWS * (s % 8)), :]
-        ahead = kv.at[:, key_rows((2 * (s // 8) + c) * BLOCK + ROWS * (s % 8)), :]
+    def source(i):
+        half = (i // 2) % 2
+        dx = (x + 4 - 2 * half - c) % 4
+        sy = (y + 8 - dx - i // 4) % 4
+        return half * 8 + sy * 2 + i % 2, (2 * half + c) * BLOCK + ROWS * (sy * 2 + i % 2)
+
+    def relay(i):
+        s, at = source(i)
+        mine = kv.at[:, key_rows(WINDOW + at), :]
+        ahead = kv.at[:, key_rows(at), :]
         bytes_of(mine, kv_sem.at[s]).wait()
 
         @pl.when(z < PLANES - 1)
@@ -236,8 +243,9 @@
 
     lax.fori_loop(1, 16, relay_send, 0)
 
-    def relay_core(s, carry):
-        mine = kv.at[:, key_rows((2 * (s // 8) + c) * BLOCK + ROWS * (s % 8)), :]
+    def relay_core(i, carry):
+        s, at = source(i)
+        mine = kv.at[:, key_rows(at), :]
         bytes_of(mine, z_sem.at[s]).wait()
         remote(mine, mine, snd_o2, o_sem, other)
         return carry
@@ -256,10 +264,6 @@
         if COMPUTE:
             unit(hd, j, at, kv, qg, first, acc, dq_st)
 
-    def first_head(j, carry):
-        run_unit(0, j)
-        return carry
-
     def tile(t):
         return acc[:, pl.ds(pl.multiple_of(t * BLOCK, BLOCK), BLOCK), :]
 
@@ -267,20 +271,26 @@
         st1[m] = tile(t).astype(BF)
         remote(st1.at[m], r1.at[m], x1_s, x1_r.at[m], other)
 
+    def half_start(h):
+        return 128 * ((1 + h + y // 2) % 2)
+
+    def half_rows(h):
+        return pl.ds(pl.multiple_of(half_start(h), 128), 128)
+
     def ship_down(i, total):
         st0[i] = total.astype(BF)
 
         @pl.when(z > 0)
         def _():
             for h in range(2):
-                part = slice(h * 128, (h + 1) * 128)
+                part = half_rows(h)
                 remote(
                     st0.at[i, :, part, :], r0.at[i, :, part, :],
                     x0_s, x0_r.at[2 * i + h], down,
                 )
 
     bytes_of(qg.at[0], qg_sem.at[0]).wait()
-    lax.fori_loop(0, 2, first_head, 0)
+    run_unit(0, 0)
     bytes_of(qg.at[1], qg_sem.at[1]).wait()
     run_unit(1, 0)
 
@@ -289,6 +299,8 @@
     @pl.when(c == 0)
     def _():
         ship_down(0, tile(0))
+
+    run_unit(0, 1)
 
     @pl.when(c == 1)
     def _():
@@ -337,17 +349,19 @@
 
     lax.fori_loop(0, 16, dq_step, 0)
 
-    def finish(j, rows, extra):
-        at = pl.ds(pl.multiple_of(WINDOW + (2 * j + c) * BLOCK + rows.start, 128), rows.stop - rows.start)
-        whole = acc[:, at, :] + r0[j, :, rows, :].astype(F32)
+    def finish(j, begin, count, extra):
+        def span(at):
+            return pl.ds(pl.multiple_of(at + begin, 128), count)
+
+        whole = acc[:, span(WINDOW + (2 * j + c) * BLOCK), :]
+        whole = whole + r0[j, :, span(0), :].astype(F32)
         if extra is not None:
-            whole = whole + extra[:, rows, :].astype(F32)
-        here = slice(j * BLOCK + rows.start, j * BLOCK + rows.stop)
-        st2[0, here, :] = (whole[0] * SCALE).astype(BF)
-        st2[1, here, :] = whole[1].astype(BF)
+            whole = whole + extra[:, span(0), :].astype(F32)
+        st2[0, span(j * BLOCK), :] = (whole[0] * SCALE).astype(BF)
+        st2[1, span(j * BLOCK), :] = whole[1].astype(BF)
 
         def step(i, carry):
-            s = j * 8 + rows.start // ROWS + i
+            s = j * 8 + begin // ROWS + i
             send_out(
                 s,
                 [
@@ -358,26 +372,25 @@
             )
             return carry
 
-        lax.fori_loop(0, (rows.stop - rows.start) // ROWS, step, 0)
-
-    bytes_of(r1.at[2], x1_r.at[2]).wait()
+        lax.fori_loop(0, count // ROWS, step, 0)
+
     def await_down(i, h):
         @pl.when(z < PLANES - 1)
         def _():
-            bytes_of(r0.at[i, :, h * 128 : (h + 1) * 128, :], x0_r.at[2 * i + h]).wait()
-
+            bytes_of(r0.at[i, :, half_rows(h), :], x0_r.at[2 * i + h]).wait()
+
+    bytes_of(r1.at[2], x1_r.at[2]).wait()
     await_down(0, 0)
     await_down(0, 1)
-    finish(0, slice(0, BLOCK), r1.at[1 + c])
+    finish(0, 0, BLOCK, r1.at[1 + c])
 
     @pl.when(c == 0)
     def _():
         acc[:, WINDOW + 2 * BLOCK : WINDOW + 3 * BLOCK, :] += r1[2].astype(F32)
 
     for h in range(2):
-        rows = slice(h * 128, (h + 1) * 128)
         await_down(1, h)
-        finish(1, rows, None)
+        finish(1, half_start(h), 128, None)
 
     bytes_of(kv.at[:, 0:1440, :], snd).wait()
 

time: 40.7 us -> 38.7 us (0.951)
  the two profiles are of different devices: /device:TPU:385 before, /device:TPU:1 now
where the time goes in v3:
time: 38.7 us; the launch traced here: 38 us
  Pallas kernels  37.4 us (97%)
  between operations  0.64 us (2%)
    pallas_call x1, Pallas kernels, per_device(): pl.pallas_call(kernel, out_shape=tuple((OUT_SHAPE(s, BF) for s in shapes)...  36.6 us
    pallas_call x1, Pallas kernels, per_device(): pl.pallas_call(put_kernel, out_shape=tuple((jax.ShapeDtypeStruct(s, BF) f...  0.81 us

profile of v3, /device:TPU:1, one launch (start us, length us, event | category | flops | bytes accessed | tf_op | source)
XLA Modules:
  0.0 38.0 jit_solution(10614689790361129083)
XLA Ops:
  0.6 36.6 %window_attention_backward.1 = (bf16[32,4096]{1,0:T(8,128)(2,1)S(1)}, bf16[32,2048]{1,0:T(8,128)(2,1)S(1)}, bf16[32,2048]{1,0:T(8,128)(2,1)S(1)}) custom-call(bf16[32,4096]{1,0:T(8,128)(2,1)} %q_hbm.1, bf16[32,2048]{1,0:T(8,128)(2,1)} %k_hbm.1, bf16[32,2048]{1,0:T(8,128)(2,1)} %v_hbm.1, bf16[32,4096]{1,0:T(8,128)(2,1)} %g_hbm.1, s32[16]{0:T(128)} %doc_hbm.1), custom_call_target="tpu_custom_call" | custom-call | tf_op jit(solution)/shard_map/window_attention_backward/pallas_call | solution.py:440
  37.2 0.8 %put_results.1 = (bf16[32,4096]{1,0:T(8,128)(2,1)}, bf16[32,2048]{1,0:T(8,128)(2,1)}, bf16[32,2048]{1,0:T(8,128)(2,1)}) custom-call(bf16[32,4096]{1,0:T(8,128)(2,1)S(1)} %get-tuple-element.6.a, bf16[32,2048]{1,0:T(8,128)(2,1)S(1)} %get-tuple-element.7.b, bf16[32,2048]{1,0:T(8,128)(2,1)S(1)} %get-tuple-element.8.d), custom_call_target="tpu_custom_call" | custom-call | tf_op jit(solution)/shard_map/put_results/pallas_call | solution.py:467

commit v4 on v3

--- a/solution.py
+++ b/solution.py
@@ -95,7 +95,7 @@
     q_hbm, k_hbm, v_hbm, g_hbm, doc_hbm,
     dq_out, dk_out, dv_out,
     kv, qg, first, acc, dq_st, st1, r1, st0, r0, st2, docs,
-    doc_sem, kv_sem, z_sem, o_sem, qg_sem, snd, snd0, snd_z, snd_o, snd_o2,
+    doc_sem, root_sem, kv_sem, z_sem, o_sem, qg_sem, snd, snd0, snd_z, snd_o, snd_o2,
     x1_s, x1_r, x0_s, x0_r, odq_s, odq_r, okv_s, odk_r, odv_r,
 ):
     seq = lax.axis_index("seq")
@@ -116,15 +116,24 @@
     barrier = pltpu.get_barrier_semaphore()
     xs = [(x + d) % 4 for d in range(4)]
     ys = [(y + d) % 4 for d in range(4)]
-    for dx, dy in sorted(
-        ((a, b) for a in range(4) for b in range(4)),
-        key=lambda p: -(min(p[0], 4 - p[0]) + min(p[1], 4 - p[1])),
-    ):
-        for tc in (1 - c, c) if (dx, dy) != (0, 0) else (1 - c,):
-            pl.semaphore_signal(
-                barrier, inc=1, device_id=(z * 4 + xs[dx], ys[dy] * 2 + tc),
-                device_id_type=MESH,
-            )
+
+    def greet(sem):
+        for dx, dy in sorted(
+            ((a, b) for a in range(4) for b in range(4)),
+            key=lambda p: -(min(p[0], 4 - p[0]) + min(p[1], 4 - p[1])),
+        ):
+            for tc in (1 - c, c) if (dx, dy) != (0, 0) else (1 - c,):
+                pl.semaphore_signal(
+                    sem, inc=1, device_id=(z * 4 + xs[dx], ys[dy] * 2 + tc),
+                    device_id_type=MESH,
+                )
+
+    root = (seq == 0) & (tp == 0)
+    beside_root = (z == 0) & jnp.logical_not(root)
+
+    @pl.when(jnp.logical_not(root))
+    def _():
+        greet(barrier)
 
     @pl.when(z < PLANES - 1)
     def _():
@@ -144,7 +153,13 @@
     def _():
         r0[...] = jnp.zeros(r0.shape, BF)
 
-    pl.semaphore_wait(barrier, 33 - z // (PLANES - 1) - (PLANES - 1 - z) // (PLANES - 1))
+    in_first = (PLANES - 1 - z) // (PLANES - 1)
+    is_root = in_first * ((3 - x) // 3) * ((7 - tp) // 7)
+    pl.semaphore_wait(barrier, 33 - z // (PLANES - 1) - 2 * in_first + is_root)
+
+    @pl.when(root)
+    def _():
+        greet(root_sem)
 
     def key_rows(at):
         return pl.ds(pl.multiple_of(at, ROWS), ROWS)
@@ -179,7 +194,7 @@
             for src, dst, sem in in_pairs(head)[kinds]:
                 pltpu.make_async_copy(src, dst, sem).start()
 
-        @pl.when(c != side)
+        @pl.when((c != side) & jnp.logical_not(beside_root & (head == 0) & (side == 0)))
         def _():
             for src, dst, sem in in_pairs(head)[kinds]:
                 remote(src, dst, snd0, sem, other)
@@ -190,11 +205,20 @@
         for src, dst, sem in in_pairs(tx * 4 + ty)[kinds]:
             remote(src, dst, snd, sem, (z * 4 + tx, ty * 2 + side))
 
+    def send_early(kinds, i):
+        tx = (x + i % 4) % 4
+        ty = (y + i % 4 + i // 4) % 4
+
+        @pl.when(jnp.logical_not((z == 0) & (tx == 0) & (ty == 0) & (side == 0)))
+        def _():
+            for src, dst, sem in in_pairs(tx * 4 + ty)[kinds]:
+                remote(src, dst, snd, sem, (z * 4 + tx, ty * 2 + side))
+
     KEYS, HEAD0, HEAD1 = slice(0, 2), slice(2, 4), slice(4, 6)
 
     def send_all(kinds):
         def step(i, carry):
-            send_away(kinds, i)
+            send_early(kinds, i)
             return carry
 
         lax.fori_loop(1, 16, step, 0)
@@ -204,6 +228,20 @@
     send_here(HEAD0)
     send_all(HEAD0)
     send_here(HEAD1)
+
+    @pl.when(beside_root)
+    def _():
+        pl.semaphore_wait(root_sem, 1)
+
+        @pl.when((side == 0) & (head != 0))
+        def _():
+            for src, dst, sem in in_pairs(0)[0:4]:
+                remote(src, dst, snd, sem, (0, 0))
+
+        @pl.when((side == 0) & (head == 0))
+        def _():
+            for src, dst, sem in in_pairs(0):
+                remote(src, dst, snd0, sem, (0, 0))
 
     doc_copy.wait()
     for j in range(2):
@@ -261,8 +299,7 @@
 
     def run_unit(hd, j):
         at = pl.multiple_of((2 * j + c) * BLOCK, BLOCK)
-        if COMPUTE:
-            unit(hd, j, at, kv, qg, first, acc, dq_st)
+        unit(hd, j, at, kv, qg, first, acc, dq_st)
 
     def tile(t):
         return acc[:, pl.ds(pl.multiple_of(t * BLOCK, BLOCK), BLOCK), :]
@@ -277,17 +314,19 @@
     def half_rows(h):
         return pl.ds(pl.multiple_of(half_start(h), 128), 128)
 
-    def ship_down(i, total):
+    def send_down(i, h):
+        @pl.when(z > 0)
+        def _():
+            part = half_rows(h)
+            remote(
+                st0.at[i, :, part, :], r0.at[i, :, part, :],
+                x0_s, x0_r.at[2 * i + h], down,
+            )
+
+    def ship_down(i, total, halves):
         st0[i] = total.astype(BF)
-
-        @pl.when(z > 0)
-        def _():
-            for h in range(2):
-                part = half_rows(h)
-                remote(
-                    st0.at[i, :, part, :], r0.at[i, :, part, :],
-                    x0_s, x0_r.at[2 * i + h], down,
-                )
+        for h in halves:
+            send_down(i, h)
 
     bytes_of(qg.at[0], qg_sem.at[0]).wait()
     run_unit(0, 0)
@@ -298,14 +337,14 @@
 
     @pl.when(c == 0)
     def _():
-        ship_down(0, tile(0))
+        ship_down(0, tile(0), (0, 1))
 
     run_unit(0, 1)
 
     @pl.when(c == 1)
     def _():
         bytes_of(r1.at[0], x1_r.at[0]).wait()
-        ship_down(0, tile(1) + r1[0].astype(F32))
+        ship_down(0, tile(1) + r1[0].astype(F32), (0, 1))
 
     run_unit(1, 1)
 
@@ -314,14 +353,7 @@
     @pl.when(c == 0)
     def _():
         bytes_of(r1.at[0], x1_r.at[0]).wait()
-        ship_down(1, tile(2) + r1[0].astype(F32))
-
-    ship_core(2, 5 + c)
-    bytes_of(r1.at[1], x1_r.at[1]).wait()
-
-    @pl.when(c == 1)
-    def _():
-        ship_down(1, tile(3) + r1[1].astype(F32))
+        ship_down(1, tile(2) + r1[0].astype(F32), (0,))
 
     own = c == side
 
@@ -347,7 +379,20 @@
         send_out(s, [(dq_st.at[key_rows(ROWS * s), :], dq_out.at[:, qcols], odq_r)], odq_s)
         return carry
 
-    lax.fori_loop(0, 16, dq_step, 0)
+    lax.fori_loop(0, 8, dq_step, 0)
+
+    @pl.when(c == 1)
+    def _():
+        bytes_of(r1.at[1], x1_r.at[1]).wait()
+        ship_down(1, tile(3) + r1[1].astype(F32), (0,))
+
+    lax.fori_loop(8, 16, dq_step, 0)
+    send_down(1, 1)
+    ship_core(2, 5 + c)
+
+    @pl.when(c == 0)
+    def _():
+        bytes_of(r1.at[1], x1_r.at[1]).wait()
 
     def finish(j, begin, count, extra):
         def span(at):
@@ -454,7 +499,7 @@
             pltpu.VMEM((2, 2, BLOCK, HEAD), BF),
             pltpu.VMEM((2, HALF, HEAD), BF),
             pltpu.SMEM((DOCS,), jnp.int32),
-            dma, dma((16,)), dma((16,)), dma, dma((2,)), dma, dma, dma, dma, dma,
+            dma, pltpu.SemaphoreType.REGULAR, dma((16,)), dma((16,)), dma, dma((2,)), dma, dma, dma, dma, dma,
             dma, dma((3,)), dma, dma((4,)), dma, dma, dma, dma, dma,
         ],
         compiler_params=pltpu.CompilerParams(
@@ -475,9 +520,6 @@
     )(*results)
 
 
-COMPUTE = True
-
-
 def solution(mesh):
     rows = P(("seq", "tp"), None)
     return jax.shard_map(

time: 38.7 us -> 37.3 us (0.964); the launches traced: 38 us -> 37.2 us
  Pallas kernels: 37.4 us -> 36.5 us
    pallas_call x1, Pallas kernels: 36.6 us -> 35.7 us  [per_device(): pl.pallas_call(kernel, out_shape=tuple((OUT_SHAPE(s, BF) for s in shapes)...]
where the time goes in v4:
time: 37.3 us; the launch traced here: 37.2 us
  Pallas kernels  36.5 us (98%)
  between operations  0.64 us (2%)
    pallas_call x1, Pallas kernels, per_device(): pl.pallas_call(kernel, out_shape=tuple((OUT_SHAPE(s, BF) for s in shapes)...  35.7 us
    pallas_call x1, Pallas kernels, per_device(): pl.pallas_call(put_kernel, out_shape=tuple((jax.ShapeDtypeStruct(s, BF) f...  0.81 us

profile of v4, /device:TPU:1, one launch (start us, length us, event | category | flops | bytes accessed | tf_op | source)
XLA Modules:
  0.0 37.2 jit_solution(9764740670222567460)
XLA Ops:
  0.6 35.7 %window_attention_backward.1 = (bf16[32,4096]{1,0:T(8,128)(2,1)S(1)}, bf16[32,2048]{1,0:T(8,128)(2,1)S(1)}, bf16[32,2048]{1,0:T(8,128)(2,1)S(1)}) custom-call(bf16[32,4096]{1,0:T(8,128)(2,1)} %q_hbm.1, bf16[32,2048]{1,0:T(8,128)(2,1)} %k_hbm.1, bf16[32,2048]{1,0:T(8,128)(2,1)} %v_hbm.1, bf16[32,4096]{1,0:T(8,128)(2,1)} %g_hbm.1, s32[16]{0:T(128)} %doc_hbm.1), custom_call_target="tpu_custom_call" | custom-call | tf_op jit(solution)/shard_map/window_attention_backward/pallas_call | solution.py:485
  36.3 0.8 %put_results.1 = (bf16[32,4096]{1,0:T(8,128)(2,1)}, bf16[32,2048]{1,0:T(8,128)(2,1)}, bf16[32,2048]{1,0:T(8,128)(2,1)}) custom-call(bf16[32,4096]{1,0:T(8,128)(2,1)S(1)} %get-tuple-element.6.a, bf16[32,2048]{1,0:T(8,128)(2,1)S(1)} %get-tuple-element.7.b, bf16[32,2048]{1,0:T(8,128)(2,1)S(1)} %get-tuple-element.8.d), custom_call_target="tpu_custom_call" | custom-call | tf_op jit(solution)/shard_map/put_results/pallas_call | solution.py:512

commit v5 on v4

--- a/solution.py
+++ b/solution.py
@@ -386,8 +386,16 @@
         bytes_of(r1.at[1], x1_r.at[1]).wait()
         ship_down(1, tile(3) + r1[1].astype(F32), (0,))
 
+    @pl.when(c == 0)
+    def _():
+        send_down(1, 1)
+
     lax.fori_loop(8, 16, dq_step, 0)
-    send_down(1, 1)
+
+    @pl.when(c == 1)
+    def _():
+        send_down(1, 1)
+
     ship_core(2, 5 + c)
 
     @pl.when(c == 0)

time: 37.3 us -> 37.3 us (level)
  no operation moved by 1% of the time
where the time goes in v5:
time: 37.3 us; the launch traced here: 37.1 us
  Pallas kernels  36.5 us (98%)
  between operations  0.64 us (2%)
    pallas_call x1, Pallas kernels, per_device(): pl.pallas_call(kernel, out_shape=tuple((OUT_SHAPE(s, BF) for s in shapes)...  35.7 us
    pallas_call x1, Pallas kernels, per_device(): pl.pallas_call(put_kernel, out_shape=tuple((jax.ShapeDtypeStruct(s, BF) f...  0.81 us

profile of v5, /device:TPU:1, one launch (start us, length us, event | category | flops | bytes accessed | tf_op | source)
XLA Modules:
  0.0 37.1 jit_solution(13389472587114615224)
XLA Ops:
  0.6 35.7 %window_attention_backward.1 = (bf16[32,4096]{1,0:T(8,128)(2,1)S(1)}, bf16[32,2048]{1,0:T(8,128)(2,1)S(1)}, bf16[32,2048]{1,0:T(8,128)(2,1)S(1)}) custom-call(bf16[32,4096]{1,0:T(8,128)(2,1)} %q_hbm.1, bf16[32,2048]{1,0:T(8,128)(2,1)} %k_hbm.1, bf16[32,2048]{1,0:T(8,128)(2,1)} %v_hbm.1, bf16[32,4096]{1,0:T(8,128)(2,1)} %g_hbm.1, s32[16]{0:T(128)} %doc_hbm.1), custom_call_target="tpu_custom_call" | custom-call | tf_op jit(solution)/shard_map/window_attention_backward/pallas_call | solution.py:493
  36.3 0.8 %put_results.1 = (bf16[32,4096]{1,0:T(8,128)(2,1)}, bf16[32,2048]{1,0:T(8,128)(2,1)}, bf16[32,2048]{1,0:T(8,128)(2,1)}) custom-call(bf16[32,4096]{1,0:T(8,128)(2,1)S(1)} %get-tuple-element.6.a, bf16[32,2048]{1,0:T(8,128)(2,1)S(1)} %get-tuple-element.7.b, bf16[32,2048]{1,0:T(8,128)(2,1)S(1)} %get-tuple-element.8.d), custom_call_target="tpu_custom_call" | custom-call | tf_op jit(solution)/shard_map/put_results/pallas_call | solution.py:520
